TPU v7x, 32 devices: a whole 2x2x4 slice. The times are simulated.
32 devices in a mesh: paths: 4 (over y, core), factors: 8 (over z, x).
Axes of the slice: x: 2, y: 2, z: 4, core: 2. Of those that a mesh axis runs over, the one named last changes fastest.
Arguments:
- x_start: float32 [512, 2048], P('factors', 'paths'), may hold values from -3 to 3
- shocks: float32 [4, 512, 2048], P(None, 'factors', 'paths'), may hold values from -6 to 6
- cholesky: float32 [512, 512], P(None, 'factors'), as said below
- reversion: float32 [512], P('factors'), may hold values from 0.05 to 2
- sabr_alpha: float32 [64], replicated, may hold values from 0.2 to 0.6
- sabr_rho: float32 [64], replicated, may hold values from -0.7 to 0.7
- sabr_nu: float32 [64], replicated, may hold values from 0.3 to 1.5
- factor_slice: int32 [512], P('factors'), may hold values from 0 to 63
- notional: float32 [32768], P('factors'), may hold values from -1 to 1
- strike: float32 [32768], P('factors'), may hold values from -3 to 3
- trade_set: int32 [32768], P('factors'), may hold values from 0 to 255
- trade_factor: int32 [32768], P('factors'), may hold values from 0 to 511, as said below
- loss_given: float32 [256], replicated, may hold values from 0.2 to 0.8
Outputs:
- path_adjoint: float32 [512, 2048], P('factors', 'paths')
- sabr_grad: float32 [3, 64], replicated
Inputs may be any that keep to these rules, and one draw needn't show every extreme that they name: `cholesky`: lower triangular with a positive diagonal and rows of unit length. `trade_factor`: trade t's factor lies in [(t // 4096) * 64, (t // 4096 + 1) * 64).
All inputs are finite; a program needn't handle non-finite values.
Results may differ from a plain program's by a relative error of at most 0.004.
Values may be sent and summed in bfloat16 or wider, within the bound.
A program may use at most 192 MiB of HBM per device.

v0:
```python
import math

import jax
import jax.numpy as jnp
from jax import lax
from jax.sharding import PartitionSpec as P

TIME_STEP = 0.25
ROOT_STEP = 0.5
DISCOUNT_RATE = 0.03
PRECISE = lax.Precision.HIGHEST
CONTRACT_FIRST = (((0,), (0,)), ((), ()))


def shortened(value):
    return jax.tree.map(lambda a: a.astype(jnp.bfloat16) if a.dtype == jnp.float32 else a, value)


def smile_terms(squashed, alpha_rows, rho_rows, nu_rows):
    curve = (2.0 - 3.0 * rho_rows * rho_rows) * nu_rows * nu_rows / 24.0
    base = 1.0 + 0.5 * rho_rows * nu_rows * squashed + curve * squashed * squashed
    rho_slope = alpha_rows * (
        0.5 * nu_rows * squashed - 0.25 * rho_rows * nu_rows * nu_rows * squashed * squashed
    )
    nu_slope = alpha_rows * (
        0.5 * rho_rows * squashed
        + (2.0 - 3.0 * rho_rows * rho_rows) * nu_rows * squashed * squashed / 12.0
    )
    level_slope = alpha_rows * (0.5 * rho_rows * nu_rows + 2.0 * curve * squashed)
    return (alpha_rows * base, base, rho_slope, nu_slope, level_slope)


def split_factors(
    x_start,
    shocks,
    cholesky,
    reversion,
    sabr_alpha,
    sabr_rho,
    sabr_nu,
    factor_slice,
    notional,
    strike,
    trade_set,
    trade_factor,
    loss_given,
):
    factor_rows, path_cols = x_start.shape
    step_count = shocks.shape[0]
    total_sets = loss_given.shape[0]
    factor_place = lax.axis_index("factors")
    slice_count = sabr_alpha.shape[0]
    slice_table = (
        factor_slice[:, None] == jnp.arange(slice_count, dtype=jnp.int32)[None, :]
    ).astype(jnp.float32)
    alpha_rows = jnp.dot(slice_table, sabr_alpha, precision=PRECISE)[:, None]
    rho_rows = jnp.dot(slice_table, sabr_rho, precision=PRECISE)[:, None]
    nu_rows = jnp.dot(slice_table, sabr_nu, precision=PRECISE)[:, None]
    local_factor = trade_factor - factor_place * factor_rows
    factor_table = (
        jnp.arange(factor_rows, dtype=jnp.int32)[:, None] == local_factor[None, :]
    ).astype(jnp.float32)
    set_table = (jnp.arange(total_sets, dtype=jnp.int32)[:, None] == trade_set[None, :]).astype(
        jnp.bfloat16
    )
    damping = (1.0 - reversion * TIME_STEP)[:, None]
    state = x_start
    states = [state]
    weights = []
    for step_index in range(step_count):
        squashed = jnp.tanh(state)
        local_vol = smile_terms(squashed, alpha_rows, rho_rows, nu_rows)[0]
        correlate_source = local_vol * shocks[step_index]
        mixed = lax.psum_scatter(
            jnp.dot(cholesky, correlate_source, precision=PRECISE),
            "factors",
            scatter_dimension=0,
            tiled=True,
        )
        state = damping * state + ROOT_STEP * mixed
        states.append(state)
        moneyness = jnp.take(state, local_factor, axis=0) - strike[:, None]
        values = (notional[:, None] * jnp.tanh(moneyness)).astype(jnp.bfloat16)
        discount = math.exp(-DISCOUNT_RATE * TIME_STEP * (step_index + 1))
        partial_sum = jnp.dot(set_table, values, preferred_element_type=jnp.float32)
        exposure = lax.psum(partial_sum.astype(jnp.bfloat16), "factors").astype(jnp.float32)
        weights.append(
            (discount * loss_given[:, None] * jax.nn.sigmoid(exposure)).astype(jnp.bfloat16)
        )
    adjoint = jnp.zeros_like(x_start)
    factor_sums = jnp.zeros((3, factor_rows), jnp.float32)
    for step_index in reversed(range(step_count)):
        moneyness = jnp.take(states[step_index + 1], local_factor, axis=0) - strike[:, None]
        squash_trade = jnp.tanh(moneyness)
        trade_term = (
            notional[:, None]
            * (1.0 - squash_trade * squash_trade)
            * lax.dot_general(
                set_table, weights[step_index], CONTRACT_FIRST, preferred_element_type=jnp.float32
            )
        )
        adjoint = adjoint + jnp.dot(factor_table, trade_term, precision=PRECISE)
        shock_adjoint = jnp.zeros((factor_rows, path_cols), jnp.float32) + lax.dot_general(
            cholesky,
            lax.all_gather(shortened(ROOT_STEP * adjoint), "factors", axis=0, tiled=True),
            CONTRACT_FIRST,
            precision=PRECISE,
        )
        squashed = jnp.tanh(states[step_index])
        local_vol, base, rho_slope, nu_slope, level_slope = smile_terms(
            squashed, alpha_rows, rho_rows, nu_rows
        )
        vol_adjoint = shock_adjoint * shocks[step_index]
        factor_sums = factor_sums + jnp.stack(
            [
                jnp.sum(vol_adjoint * base, axis=1),
                jnp.sum(vol_adjoint * rho_slope, axis=1),
                jnp.sum(vol_adjoint * nu_slope, axis=1),
            ]
        )
        adjoint = damping * adjoint + vol_adjoint * level_slope * (1.0 - squashed * squashed)
    slice_sums = jnp.dot(factor_sums, slice_table, precision=PRECISE)
    return (adjoint, slice_sums)


def per_device(
    x_start,
    shocks,
    cholesky,
    reversion,
    sabr_alpha,
    sabr_rho,
    sabr_nu,
    factor_slice,
    notional,
    strike,
    trade_set,
    trade_factor,
    loss_given,
):
    adjoint, slice_sums = split_factors(
        x_start,
        shocks,
        cholesky,
        reversion,
        sabr_alpha,
        sabr_rho,
        sabr_nu,
        factor_slice,
        notional,
        strike,
        trade_set,
        trade_factor,
        loss_given,
    )
    total_grad = lax.psum(slice_sums, ("paths", "factors"))
    sabr_grad = total_grad / (x_start.shape[1] * lax.axis_size("paths"))
    return (adjoint, sabr_grad)


def solution(mesh):
    return jax.shard_map(
        per_device,
        mesh=mesh,
        in_specs=(
            P("factors", "paths"),
            P(None, "factors", "paths"),
            P(None, "factors"),
            P("factors"),
            P(),
            P(),
            P(),
            P("factors"),
            P("factors"),
            P("factors"),
            P("factors"),
            P("factors"),
            P(),
        ),
        out_specs=(P("factors", "paths"), P()),
        check_vma=False,
    )
```

profile of v0, /device:TPU:0, one launch (start us, length us, event | category | flops | bytes accessed | tf_op | source)
XLA Modules:
  0.0 587.8 jit_solution(14679514657513539477)
XLA Ops:
  10.0 2.1 convolution_bitcast_fusion.3
  12.1 1.3 copy.39
  14.2 66.8 %reduce-scatter.13.cloned.1.call-done = f32[64,512]{1,0:T(8,128)} async-done(((f32[512,512]{1,0:T(8,128)}), f32[64,512]{1,0:T(8,128)}) %reduce-scatter.13.cloned.1.call-update) | async-done | bytes 131088 | tf_op jit(solution)/shard_map/reduce_scatter | solution.py:74
  82.0 2.0 convolution_bitcast_fusion.2
  85.4 63.7 %reduce-scatter.15.cloned.1.call-done = f32[64,512]{1,0:T(8,128)} async-done(((f32[512,512]{1,0:T(8,128)}), f32[64,512]{1,0:T(8,128)}) %reduce-scatter.15.cloned.1.call-update) | async-done | bytes 131088 | tf_op jit(solution)/shard_map/reduce_scatter | solution.py:74
  151.2 1.4 copy.43
  152.8 16.8 %gather_fusion.3 = f32[4096,512]{1,0:T(8,128)} fusion(f32[64,512]{1,0:T(8,128)S(1)} %multiply_add_fusion.4, s32[4096]{0:T(1024)S(1)} %fusion.166), kind=kCustom, calls=%fused_computation.3.clone | custom fusion | bytes 16793600 | tf_op jit(solution)/shard_map/jit(_take)/gather | solution.py:93
  169.5 46.3 %reduce-scatter.17.cloned.1.call-done = f32[64,512]{1,0:T(8,128)} async-done(((f32[512,512]{1,0:T(8,128)}), f32[64,512]{1,0:T(8,128)}) %reduce-scatter.17.cloned.1.call-update) | async-done | bytes 131088 | tf_op jit(solution)/shard_map/reduce_scatter | solution.py:74
  217.9 1.4 copy.45
  220.0 6.3 %fusion.67 = bf16[256,512]{1,0:T(8,128)(2,1)} fusion(f32[4096,512]{1,0:T(8,128)} %gather_fusion.3, f32[4096]{0:T(1024)S(1)} %copy-done.10, f32[4096]{0:T(1024)S(1)} %copy-done.11, pred[4096]{0:T(1024)(128)(4,1)S(1)} %get-tuple-element.32, s32[4096]{0:T(1024)S(1)} %copy-done.3), kind=kOutput, calls=%fused_computation.80 | convolution fusion | flops 1083310080 | bytes 8704000 | tf_op jit(solution)/shard_map/dot_general | solution.py:85
  226.3 16.8 %gather_fusion.2 = f32[4096,512]{1,0:T(8,128)} fusion(f32[64,512]{1,0:T(8,128)S(1)} %multiply_add_fusion.3, s32[4096]{0:T(1024)S(1)} %fusion.166), kind=kCustom, calls=%fused_computation.2.clone | custom fusion | bytes 16793600 | tf_op jit(solution)/shard_map/jit(_take)/gather | solution.py:93
  243.1 6.3 %fusion.66 = bf16[256,512]{1,0:T(8,128)(2,1)} fusion(f32[4096,512]{1,0:T(8,128)} %gather_fusion.2, f32[4096]{0:T(1024)S(1)} %copy-done.10, f32[4096]{0:T(1024)S(1)} %copy-done.11, pred[4096]{0:T(1024)(128)(4,1)S(1)} %get-tuple-element.32, s32[4096]{0:T(1024)S(1)} %copy-done.3), kind=kOutput, calls=%fused_computation.79 | convolution fusion | flops 1083310080 | bytes 8704000 | tf_op jit(solution)/shard_map/dot_general | solution.py:85
  249.4 16.8 %gather_fusion.1 = f32[4096,512]{1,0:T(8,128)} fusion(f32[64,512]{1,0:T(8,128)S(1)} %multiply_add_fusion.2, s32[4096]{0:T(1024)S(1)} %fusion.166), kind=kCustom, calls=%fused_computation.1.clone | custom fusion | bytes 16793600 | tf_op jit(solution)/shard_map/jit(_take)/gather | solution.py:93
  266.2 6.3 %fusion.65 = bf16[256,512]{1,0:T(8,128)(2,1)} fusion(f32[4096,512]{1,0:T(8,128)} %gather_fusion.1, f32[4096]{0:T(1024)S(1)} %copy-done.10, f32[4096]{0:T(1024)S(1)} %copy-done.11, pred[4096]{0:T(1024)(128)(4,1)S(1)} %get-tuple-element.32, s32[4096]{0:T(1024)S(1)} %copy-done.3), kind=kOutput, calls=%fused_computation.78 | convolution fusion | flops 1083310080 | bytes 8704000 | tf_op jit(solution)/shard_map/dot_general | solution.py:85
  272.5 10.2 %reduce-scatter.19.cloned.1.call-done = f32[64,512]{1,0:T(8,128)} async-done(((f32[512,512]{1,0:T(8,128)}), f32[64,512]{1,0:T(8,128)}) %reduce-scatter.19.cloned.1.call-update) | async-done | bytes 131088 | tf_op jit(solution)/shard_map/reduce_scatter | solution.py:74
  283.7 16.8 %gather_fusion = f32[4096,512]{1,0:T(8,128)} fusion(f32[64,512]{1,0:T(8,128)S(1)} %multiply_add_fusion.1, s32[4096]{0:T(1024)S(1)} %fusion.166), kind=kCustom, calls=%fused_computation.clone | custom fusion | bytes 16793600 | tf_op jit(solution)/shard_map/jit(_take)/gather | solution.py:93
  300.5 6.3 %fusion.64 = bf16[256,512]{1,0:T(8,128)(2,1)} fusion(f32[4096,512]{1,0:T(8,128)} %gather_fusion, f32[4096]{0:T(1024)S(1)} %copy-done.10, f32[4096]{0:T(1024)S(1)} %copy-done.11, pred[4096]{0:T(1024)(128)(4,1)S(1)} %get-tuple-element.32, s32[4096]{0:T(1024)S(1)} %copy-done.3), kind=kOutput, calls=%fused_computation.77 | convolution fusion | flops 1083310080 | bytes 8704000 | tf_op jit(solution)/shard_map/dot_general | solution.py:85
  306.9 77.5 %all-reduce.3.cloned.1.call-done = (bf16[256,512]{1,0:T(8,128)(2,1)}, bf16[256,512]{1,0:T(8,128)(2,1)}, bf16[256,512]{1,0:T(8,128)(2,1)}, bf16[256,512]{1,0:T(8,128)(2,1)}) async-done(((bf16[256,512]{1,0:T(8,128)(2,1)}, bf16[256,512]{1,0:T(8,128)(2,1)}, bf16[256,512]{1,0:T(8,128)(2,1)}, bf16[256,512]{1,0:T(8,128)(2,1)}), (bf16[256,512]{1,0:T(8,128)(2,1)}, bf16[256,512]{1,0:T(8,128)(2,1)}, ...) | async-done | bytes 1048592 | tf_op jit(solution)/shard_map/psum | solution.py:86
  384.4 2.5 fusion.38
  387.9 5.4 multiply_convert_fusion.27
  393.2 31.5 %all_gather.12 = bf16[512,512]{1,0:T(8,128)(2,1)S(1)} all-gather(bf16[64,512]{1,0:T(8,128)(2,1)S(1)} %get-tuple-element.45), channel_id=1, replica_groups=mesh['paths'=4,'factors'=8] {'factors'}, dimensions={0}, use_global_device_ids=true | all-gather | bytes 589824 | tf_op jit(solution)/shard_map/all_gather | solution.py:105
  425.1 1.4 fusion.36
  426.5 5.4 multiply_convert_fusion.26
  431.9 31.6 %all_gather.13 = bf16[512,512]{1,0:T(8,128)(2,1)S(1)} all-gather(bf16[64,512]{1,0:T(8,128)(2,1)S(1)} %get-tuple-element.47), channel_id=1, replica_groups=mesh['paths'=4,'factors'=8] {'factors'}, dimensions={0}, use_global_device_ids=true | all-gather | bytes 589824 | tf_op jit(solution)/shard_map/all_gather | solution.py:105
  463.9 1.4 fusion.34
  465.4 5.4 multiply_convert_fusion.25
  470.7 31.5 %all_gather.14 = bf16[512,512]{1,0:T(8,128)(2,1)S(1)} all-gather(bf16[64,512]{1,0:T(8,128)(2,1)S(1)} %get-tuple-element.49), channel_id=1, replica_groups=mesh['paths'=4,'factors'=8] {'factors'}, dimensions={0}, use_global_device_ids=true | all-gather | bytes 589824 | tf_op jit(solution)/shard_map/all_gather | solution.py:105
  502.6 1.4 fusion.32
  504.1 5.4 multiply_convert_fusion.24
  509.5 31.2 %all_gather.15 = bf16[512,512]{1,0:T(8,128)(2,1)S(1)} all-gather(bf16[64,512]{1,0:T(8,128)(2,1)S(1)} %get-tuple-element.51), channel_id=1, replica_groups=mesh['paths'=4,'factors'=8] {'factors'}, dimensions={0}, use_global_device_ids=true | all-gather | bytes 589824 | tf_op jit(solution)/shard_map/all_gather | solution.py:105
  540.6 1.6 fusion.100
  542.5 37.9 %psum.39 = f32[3,64]{1,0:T(4,128)S(1)} all-reduce(f32[3,64]{1,0:T(4,128)S(1)} %fusion.161), channel_id=1, replica_groups=mesh['paths'=4,'factors'=8] {'paths','factors'}, use_global_device_ids=true, to_apply=%region_20.22 | all-reduce | flops 192 | bytes 1536 | tf_op jit(solution)/shard_map/psum | solution.py:156
  (71 shorter events, 14.8 us)
Async XLA Ops:
  7.2 2.8 copy-start
  7.2 142.9 %copy-start.2 = (f32[4,64,512]{2,1,0:T(8,128)S(1)}, f32[4,64,512]{2,1,0:T(8,128)}, u32[]{:S(2)}) copy-start(f32[4,64,512]{2,1,0:T(8,128)} %param.16) | copy-start | bytes 1572868
  7.2 145.5 %copy-start.8 = (s32[4096]{0:T(1024)S(1)}, s32[4096]{0:T(1024)}, u32[]{:S(2)}) copy-start(s32[4096]{0:T(1024)} %param.26) | copy-start | bytes 49156
  7.2 73.7 %reduce-scatter.13.cloned.1.call-start = ((), (), s32[]{:S(2)}) async-start(), calls=%async_computation.4 | async-start | bytes 1179648 | tf_op jit(solution)/shard_map/reduce_scatter | solution.py:74
  13.4 135.6 %reduce-scatter.15.cloned.1.call-start = ((), (), s32[]{:S(2)}) async-start(), calls=%async_computation.5 | async-start | bytes 1179648 | tf_op jit(solution)/shard_map/reduce_scatter | solution.py:74
  85.4 130.4 %reduce-scatter.17.cloned.1.call-start = ((), (), s32[]{:S(2)}) async-start(), calls=%async_computation.6 | async-start | bytes 1179648 | tf_op jit(solution)/shard_map/reduce_scatter | solution.py:74
  152.6 130.1 %reduce-scatter.19.cloned.1.call-start = ((), (), s32[]{:S(2)}) async-start(), calls=%async_computation.7 | async-start | bytes 1179648 | tf_op jit(solution)/shard_map/reduce_scatter | solution.py:74
  152.7 67.2 %copy-start.3 = (s32[4096]{0:T(1024)S(1)}, s32[4096]{0:T(1024)}, u32[]{:S(2)}) copy-start(s32[4096]{0:T(1024)} %param.25) | copy-start | bytes 49156
  152.7 67.2 %copy-start.10 = (f32[4096]{0:T(1024)S(1)}, f32[4096]{0:T(1024)}, u32[]{:S(2)}) copy-start(f32[4096]{0:T(1024)} %param.24) | copy-start | bytes 49156
  152.7 67.2 %copy-start.11 = (f32[4096]{0:T(1024)S(1)}, f32[4096]{0:T(1024)}, u32[]{:S(2)}) copy-start(f32[4096]{0:T(1024)} %param.23) | copy-start | bytes 49156
  219.3 165.1 %all-reduce.3.cloned.1.call-start = ((), (), s32[]{:S(2)}) async-start(), calls=%async_computation.8 | async-start | bytes 2097152 | tf_op jit(solution)/shard_map/psum | solution.py:86
  300.5 6.4 %copy-start.9 = (f32[256]{0:T(256)S(1)}, f32[256]{0:T(256)}, u32[]{:S(2)}) copy-start(f32[256]{0:T(256)} %param.27) | copy-start | bytes 3076
  384.4 3.5 copy-start.1
  384.4 42.1 %slice-start.4 = ((s8[8388608]{0:T(1024)(128)(4,1)}), s8[4194304]{0:T(1024)(128)(4,1)S(1)}, s32[]{:S(2)}) async-start(s8[8388608]{0:T(1024)(128)(4,1)} %bitcast.89), calls=%async_computation.13 | async-start | bytes 8388608
  387.9 37.2 %copy-start.7 = (bf16[256,512]{1,0:T(8,128)(2,1)S(1)}, bf16[256,512]{1,0:T(8,128)(2,1)}, u32[]{:S(2)}) copy-start(bf16[256,512]{1,0:T(8,128)(2,1)} %get-tuple-element.28) | copy-start | bytes 786436
  387.9 38.6 %slice-start.5 = ((s8[8388608]{0:T(1024)(128)(4,1)}), s8[4194304]{0:T(1024)(128)(4,1)S(1)}, s32[]{:S(2)}) async-start(s8[8388608]{0:T(1024)(128)(4,1)} %bitcast.89), calls=%async_computation.14 | async-start | bytes 8388608
  426.5 38.8 %slice-start.2 = ((s8[8388608]{0:T(1024)(128)(4,1)}), s8[4194304]{0:T(1024)(128)(4,1)S(1)}, s32[]{:S(2)}) async-start(s8[8388608]{0:T(1024)(128)(4,1)} %bitcast.87), calls=%async_computation.11 | async-start | bytes 8388608
  426.5 37.4 %copy-start.6 = (bf16[256,512]{1,0:T(8,128)(2,1)S(1)}, bf16[256,512]{1,0:T(8,128)(2,1)}, u32[]{:S(2)}) copy-start(bf16[256,512]{1,0:T(8,128)(2,1)} %get-tuple-element.27) | copy-start | bytes 786436
  426.5 38.8 %slice-start.3 = ((s8[8388608]{0:T(1024)(128)(4,1)}), s8[4194304]{0:T(1024)(128)(4,1)S(1)}, s32[]{:S(2)}) async-start(s8[8388608]{0:T(1024)(128)(4,1)} %bitcast.87), calls=%async_computation.12 | async-start | bytes 8388608
  465.3 38.7 %slice-start = ((s8[8388608]{0:T(1024)(128)(4,1)}), s8[4194304]{0:T(1024)(128)(4,1)S(1)}, s32[]{:S(2)}) async-start(s8[8388608]{0:T(1024)(128)(4,1)} %bitcast.85), calls=%async_computation.9 | async-start | bytes 8388608
  465.4 37.3 %copy-start.5 = (bf16[256,512]{1,0:T(8,128)(2,1)S(1)}, bf16[256,512]{1,0:T(8,128)(2,1)}, u32[]{:S(2)}) copy-start(bf16[256,512]{1,0:T(8,128)(2,1)} %get-tuple-element.26) | copy-start | bytes 786436
  465.4 38.7 %slice-start.1 = ((s8[8388608]{0:T(1024)(128)(4,1)}), s8[4194304]{0:T(1024)(128)(4,1)S(1)}, s32[]{:S(2)}) async-start(s8[8388608]{0:T(1024)(128)(4,1)} %bitcast.85), calls=%async_computation.10 | async-start | bytes 8388608
  504.1 36.6 %copy-start.4 = (f32[64,512]{1,0:T(8,128)S(1)}, f32[64,512]{1,0:T(8,128)}, u32[]{:S(2)}) copy-start(f32[64,512]{1,0:T(8,128)} %param.15) | copy-start | bytes 393220
  504.1 38.2 %copy-start.12 = (s32[64]{0:T(128)S(1)}, s32[64]{0:T(128)}, u32[]{:S(2)}) copy-start(s32[64]{0:T(128)} %param.22) | copy-start | bytes 772
Sparse Core Ops, SparseCore 0:
  13.6 67.3 reduce-scatter.12
  85.5 63.5 reduce-scatter.14
  152.7 63.0 reduce-scatter.16
  219.5 63.1 reduce-scatter.18
  307.0 77.3 all-reduce.2
where the time goes:
time: 593 us; the launch traced here: 588 us
  waiting for transfers between devices  264 us (45%)
  blocking collectives  164 us (28%)
  local copies, waits for them, and re-layouts  73.7 us (12%)
  matrix products  65.4 us (11%)
  between operations  14.5 us (2%)
    reduce_scatter x4, waiting for transfers between devices, split_factors(): lax.psum_scatter(jnp.dot(cholesky, correlate_source, precision=PRECISE),...  187 us
    all_gather x4, blocking collectives, split_factors(): lax.all_gather(shortened(ROOT_STEP * adjoint), 'factors', axis=0, tiled=T...  126 us
    psum x1, waiting for transfers between devices, split_factors(): lax.psum(partial_sum.astype(jnp.bfloat16), 'factors').astype(jnp.float32)  77.5 us
    gather x4, local copies, waits for them, and re-layouts, split_factors(): jnp.take(states[step_index + 1], local_factor, axis=0) - strike[:, None]  67.2 us
    psum x1, blocking collectives, per_device(): total_grad = lax.psum(slice_sums, ('paths', 'factors'))  37.9 us
    dot_general x4, matrix products, split_factors(): partial_sum = jnp.dot(set_table, values, preferred_element_type=jnp.float32)  25.3 us
    dot_general x4, matrix products, split_factors(): adjoint = adjoint + jnp.dot(factor_table, trade_term, precision=PRECISE)  21.4 us
  transfers between devices with their start and end apart: 5, of which 5 were waited for; matrix products, arithmetic and copies ran while one was open for 12% of the time, Pallas kernels for 0%

commit v1 on v0

v1 whole, which is shorter than its diff:
```python
import functools
import math

import jax
import jax.numpy as jnp
from jax import lax
from jax.experimental import pallas as pl
from jax.experimental.pallas import tpu as pltpu
from jax.sharding import PartitionSpec as P

TIME_STEP = 0.25
ROOT_STEP = 0.5
DISCOUNT_RATE = 0.03
PRECISE = lax.Precision.HIGHEST
NN = (((1,), (0,)), ((), ()))
NT = (((1,), (1,)), ((), ()))
TILE = 512


def mm(a, b, dims):
    return lax.dot_general(a, b, dims, preferred_element_type=jnp.float32)


def split_mm(a, b, dims):
    rows = a.shape[0]
    high = a.astype(jnp.bfloat16)
    low = (a - high.astype(jnp.float32)).astype(jnp.bfloat16)
    both = mm(jnp.concatenate([high, low], axis=0), b, dims)
    return both[:rows] + both[rows:]


def one_hot(ids, count):
    rows = lax.broadcasted_iota(jnp.int32, (count, ids.shape[1]), 0).astype(jnp.float32)
    return jnp.where(rows == ids, 1.0, 0.0).astype(jnp.bfloat16)


def local_kernel(
    xs_ref,
    lt_ref,
    par_ref,
    trades_ref,
    loss_ref,
    a_ref,
    g_ref,
    states,
    parts,
    slopes,
    exposure,
    terms,
):
    steps = xs_ref.shape[0] - 1
    paths = xs_ref.shape[1]
    blocks, rows, part_width = parts.shape
    width = part_width // 3
    tiles = trades_ref.shape[0]
    per_block = tiles // blocks
    sets = loss_ref.shape[1]
    slices = g_ref.shape[1]

    alpha, rho, nu = par_ref[0:1, :], par_ref[1:2, :], par_ref[2:3, :]
    damping = 1.0 - par_ref[3:4, :] * TIME_STEP
    curve2 = 2.0 - 3.0 * rho * rho
    curve = curve2 * nu * nu / 24.0
    tilt = 0.5 * rho * nu

    state = xs_ref[0]
    for k in range(steps):
        states[k] = state
        u = jnp.tanh(state)
        source = alpha * (1.0 + tilt * u + curve * u * u) * xs_ref[k + 1]
        state = damping * state + ROOT_STEP * split_mm(source, lt_ref[...], NN)
        high = state.astype(jnp.bfloat16)
        rest = state - high.astype(jnp.float32)
        mid = rest.astype(jnp.bfloat16)
        low = (rest - mid.astype(jnp.float32)).astype(jnp.bfloat16)
        for b in range(blocks):
            cols = slice(b * width, (b + 1) * width)
            parts[b, k * paths : (k + 1) * paths, :] = jnp.concatenate(
                [high[:, cols], mid[:, cols], low[:, cols]], axis=1
            )

    exposure[...] = jnp.zeros_like(exposure)

    def forward(i, carry):
        b = i // per_block
        notional = trades_ref[i, 0:1, :]
        strike = trades_ref[i, 1:2, :]
        table = one_hot(trades_ref[i, 3:4, :], width)
        money = mm(parts[b], jnp.concatenate([table, table, table], axis=0), NN) - strike
        squash = jnp.tanh(money)
        value = notional * squash
        slopes[i] = (notional - value * squash).astype(jnp.bfloat16)
        set_table = one_hot(trades_ref[i, 2:3, :], sets)
        exposure[...] += mm(value.astype(jnp.bfloat16), set_table, NT)
        return carry

    lax.fori_loop(0, tiles, forward, 0)

    weights = jnp.concatenate(
        [
            math.exp(-DISCOUNT_RATE * TIME_STEP * (k + 1))
            * loss_ref[...]
            * jax.nn.sigmoid(exposure[k * paths : (k + 1) * paths, :])
            for k in range(steps)
        ],
        axis=0,
    ).astype(jnp.bfloat16)
    terms[...] = jnp.zeros_like(terms)

    def backward(i, carry):
        b = i // per_block
        set_table = one_hot(trades_ref[i, 2:3, :], sets)
        pulled = slopes[i].astype(jnp.float32) * mm(weights, set_table, NN)
        table = one_hot(trades_ref[i, 3:4, :], width)
        terms[b] += mm(pulled.astype(jnp.bfloat16), table, NT)
        return carry

    lax.fori_loop(0, tiles, backward, 0)

    adjoint = jnp.zeros_like(state)
    sums = [jnp.zeros((1, state.shape[1]), jnp.float32) for _ in range(3)]
    for k in reversed(range(steps)):
        adjoint = adjoint + jnp.concatenate(
            [terms[b, k * paths : (k + 1) * paths, :] for b in range(blocks)], axis=1
        )
        u = jnp.tanh(states[k])
        vbar = split_mm(ROOT_STEP * adjoint, lt_ref[...], NT) * xs_ref[k + 1]
        for at, slope in enumerate(
            (
                1.0 + tilt * u + curve * u * u,
                alpha * (0.5 * nu * u - 0.25 * rho * nu * nu * u * u),
                alpha * (0.5 * rho * u + curve2 * nu * u * u / 12.0),
            )
        ):
            sums[at] = sums[at] + jnp.sum(vbar * slope, axis=0, keepdims=True)
        adjoint = damping * adjoint + vbar * (alpha * (tilt + 2.0 * curve * u)) * (1.0 - u * u)
    a_ref[...] = adjoint
    zero = jnp.zeros((5, state.shape[1]), jnp.float32)
    slice_ids = par_ref[4:5, :]
    slice_rows = lax.broadcasted_iota(jnp.int32, (slices, state.shape[1]), 0).astype(jnp.float32)
    slice_table = jnp.where(slice_rows == slice_ids, 1.0, 0.0)
    g_ref[...] = lax.dot_general(
        jnp.concatenate(sums + [zero], axis=0),
        slice_table,
        NT,
        precision=PRECISE,
        preferred_element_type=jnp.float32,
    )


def local_part(xs, lt, params, trades, loss_given, width, slices):
    steps, paths, factors = xs.shape[0] - 1, xs.shape[1], xs.shape[2]
    blocks = factors // width
    tiles, _, tile = trades.shape
    rows, sets = steps * paths, loss_given.shape[0]
    return pl.pallas_call(
        local_kernel,
        out_shape=(
            jax.ShapeDtypeStruct((paths, factors), jnp.float32),
            jax.ShapeDtypeStruct((8, slices), jnp.float32),
        ),
        in_specs=[pl.BlockSpec(memory_space=pltpu.VMEM)] * 5,
        out_specs=(pl.BlockSpec(memory_space=pltpu.VMEM),) * 2,
        scratch_shapes=[
            pltpu.VMEM((steps, paths, factors), jnp.float32),
            pltpu.VMEM((blocks, rows, 3 * width), jnp.bfloat16),
            pltpu.VMEM((tiles, rows, tile), jnp.bfloat16),
            pltpu.VMEM((rows, sets), jnp.float32),
            pltpu.VMEM((blocks, rows, width), jnp.float32),
        ],
        compiler_params=pltpu.CompilerParams(vmem_limit_bytes=56 * 1024 * 1024),
    )(xs, lt, params, trades, loss_given[None, :])


def per_device(
    x_start,
    shocks,
    cholesky,
    reversion,
    sabr_alpha,
    sabr_rho,
    sabr_nu,
    factor_slice,
    notional,
    strike,
    trade_set,
    trade_factor,
    loss_given,
):
    width, path_cols = x_start.shape
    steps = shocks.shape[0]
    groups = lax.axis_size("factors")
    paths = path_cols // groups
    slice_count = sabr_alpha.shape[0]
    tile = min(TILE, notional.shape[0])
    floats = jnp.float32

    slice_table = (factor_slice[None, :] == jnp.arange(slice_count, dtype=jnp.int32)[:, None]).astype(
        floats
    )
    smile = jnp.dot(jnp.stack([sabr_alpha, sabr_rho, sabr_nu]), slice_table, precision=PRECISE)
    params = jnp.concatenate([smile, reversion[None, :], factor_slice.astype(floats)[None, :]], axis=0)
    params = jnp.pad(params, ((0, 3), (0, 0)))
    params = lax.all_gather(params, "factors", axis=1, tiled=True)

    local_factor = trade_factor - lax.axis_index("factors") * width
    trades = jnp.stack(
        [a.astype(floats).reshape(-1, tile) for a in (notional, strike, trade_set, local_factor)],
        axis=1,
    )
    trades = lax.all_gather(trades, "factors", axis=0, tiled=True)
    lt = lax.all_gather(cholesky.T.astype(jnp.bfloat16), "factors", axis=0, tiled=True)

    xs = jnp.concatenate([x_start[None], shocks], axis=0)
    xs = xs.reshape(steps + 1, width, groups, paths).transpose(2, 0, 3, 1)
    xs = lax.all_to_all(xs.reshape(groups, -1, 128), "factors", 0, 0, tiled=True)
    xs = xs.reshape(groups, steps + 1, paths, width).transpose(1, 2, 0, 3)
    xs = xs.reshape(steps + 1, paths, groups * width)

    adjoint, grads = local_part(xs, lt, params, trades, loss_given, width, slice_count)

    back = adjoint.reshape(paths, groups, width).transpose(1, 2, 0)
    back = lax.all_to_all(back.reshape(groups, -1, 128), "factors", 0, 0, tiled=True)
    back = back.reshape(groups, width, paths).transpose(1, 0, 2).reshape(width, path_cols)
    total = lax.psum(grads[:3], ("paths", "factors"))
    return back, total / (path_cols * lax.axis_size("paths"))


def solution(mesh):
    return jax.shard_map(
        per_device,
        mesh=mesh,
        in_specs=(
            P("factors", "paths"),
            P(None, "factors", "paths"),
            P(None, "factors"),
            P("factors"),
            P(),
            P(),
            P(),
            P("factors"),
            P("factors"),
            P("factors"),
            P("factors"),
            P("factors"),
            P(),
        ),
        out_specs=(P("factors", "paths"), P()),
        check_vma=False,
    )
```

time: 593 us -> 223 us (0.38)
  waiting for transfers between devices: 264 us -> 0.01 us
  matrix products: 65.4 us -> 0.13 us
  local copies, waits for them, and re-layouts: 73.7 us -> 9.75 us
  Pallas kernels: 0 us -> 53.7 us
  blocking collectives: 164 us -> 147 us
  between operations: 14.5 us -> 0.88 us
  starting transfers between devices: 0.73 us -> 10.8 us
    reduce_scatter x4 -> x0, waiting for transfers between devices: 187 us -> none  [split_factors(): lax.psum_scatter(jnp.dot(cholesky, correlate_source, precision=PRECISE),...]
    psum x1 -> x0, waiting for transfers between devices: 77.5 us -> none  [split_factors(): lax.psum(partial_sum.astype(jnp.bfloat16), 'factors').astype(jnp.float32)]
    gather x4 -> x0, local copies, waits for them, and re-layouts: 67.2 us -> none  [split_factors(): jnp.take(states[step_index + 1], local_factor, axis=0) - strike[:, None]]
    dot_general x24 -> x1, matrix products: 65.4 us -> 0.13 us  [per_device(): jnp.dot(jnp.stack([sabr_alpha, sabr_rho, sabr_nu]), slice_table, precisio...]
    pallas_call x0 -> x1, Pallas kernels: none -> 53.7 us  [local_part(): pl.pallas_call(local_kernel, out_shape=(jax.ShapeDtypeStruct((paths, fact...]
    all_gather x4 -> x3, blocking collectives: 126 us -> 106 us  [the longest x1 39.2 us: per_device(): params = lax.all_gather(params, 'factors', axis=1, tiled=True)]
    all_to_all x0 -> x2, starting transfers between devices: none -> 10.8 us  [the longest x1 7.41 us: per_device(): lax.all_to_all(xs.reshape(groups, -1, 128), 'factors', 0, 0, tiled=True)]
  transfers between devices with their start and end apart: 5 -> 2, of which waited for: 5 -> 0; matrix products, arithmetic and copies ran while one was open for 12% -> 1% of each run, Pallas kernels for 0% -> 0%
where the time goes in v1:
time: 223 us
  blocking collectives  147 us (66%)
  Pallas kernels  53.7 us (24%)
  starting transfers between devices  10.8 us (5%)
  local copies, waits for them, and re-layouts  9.75 us (4%)
    pallas_call x1, Pallas kernels, local_part(): pl.pallas_call(local_kernel, out_shape=(jax.ShapeDtypeStruct((paths, fact...  53.7 us
    psum x1, blocking collectives, per_device(): total = lax.psum(grads[:3], ('paths', 'factors'))  40.6 us
    all_gather x1, blocking collectives, per_device(): params = lax.all_gather(params, 'factors', axis=1, tiled=True)  39.2 us
    all_gather x1, blocking collectives, per_device(): trades = lax.all_gather(trades, 'factors', axis=0, tiled=True)  33.7 us
    all_gather x1, blocking collectives, per_device(): lax.all_gather(cholesky.T.astype(jnp.bfloat16), 'factors', axis=0, tiled=...  33.4 us
    all_to_all x1, starting transfers between devices, per_device(): lax.all_to_all(xs.reshape(groups, -1, 128), 'factors', 0, 0, tiled=True)  7.41 us
  transfers between devices with their start and end apart: 2, of which 0 were waited for; matrix products, arithmetic and copies ran while one was open for 1% of the time, Pallas kernels for 0%

profile of v1, /device:TPU:0, one launch (start us, length us, event | category | flops | bytes accessed | tf_op | source)
XLA Modules:
  0.0 222.9 jit_solution(18191158505504818917)
XLA Ops:
  0.6 1.2 concatenate.12
  1.9 0.0 copy-start
  1.9 0.4 copy.28
  2.3 0.5 copy-done
  2.8 0.1 copy.33
  2.9 0.2 maximum_bitcast_fusion
  3.1 0.0 copy-start.7
  3.1 0.0 copy-start.9
  3.1 0.0 copy-start.10
  3.2 0.0 copy-start.3
  3.2 0.0 copy-start.4
  3.2 1.1 reshape.30
  4.3 7.4 %all-to-all-start = ((f32[8,160,128]{2,1,0:T(8,128)}), f32[8,160,128]{2,1,0:T(8,128)S(1)}, u32[]{:S(2)}, u32[]{:S(2)}) async-start(f32[8,160,128]{2,1,0:T(8,128)} %reshape.30), calls=%async_computation | async-start | bytes 1310720 | tf_op jit(solution)/shard_map/all_to_all | solution.py:216
  11.7 0.1 fusion
  11.9 39.2 %all-gather = f32[8,64,8]{1,2,0:T(8,128)S(1)} all-gather(f32[1,64,8]{1,2,0:T(8,128)S(1)} %fusion.2), channel_id=1, replica_groups=mesh['paths'=4,'factors'=8] {'factors'}, dimensions={0}, use_global_device_ids=true | all-gather | bytes 18432 | tf_op jit(solution)/shard_map/all_gather | solution.py:204
  51.1 0.7 reshape.38
  51.8 0.1 pad_maximum_fusion
  51.9 33.7 %all_gather.11.trades_ref = f32[64,4,512]{2,1,0:T(4,128)} all-gather(f32[8,4,512]{2,1,0:T(4,128)S(1)} %pad_maximum_fusion), channel_id=1, replica_groups=mesh['paths'=4,'factors'=8] {'factors'}, dimensions={0}, use_global_device_ids=true | all-gather | bytes 589824 | tf_op jit(solution)/shard_map/all_gather | solution.py:211
  85.6 33.4 %all_gather.9.lt_ref = bf16[512,512]{1,0:T(8,128)(2,1)} all-gather(bf16[64,512]{1,0:T(8,128)(2,1)S(1)} %convert_bitcast_fusion), channel_id=1, replica_groups=mesh['paths'=4,'factors'=8] {'factors'}, dimensions={0}, use_global_device_ids=true | all-gather | bytes 589824 | tf_op jit(solution)/shard_map/all_gather | solution.py:212
  119.0 0.2 reshape.31
  119.2 0.7 copy.29
  120.0 1.2 reshape.32.xs_ref
  121.2 53.7 %shard_map.140 = (f32[64,512]{1,0:T(8,128)}, f32[8,64]{1,0:T(8,128)}) custom-call(f32[5,64,512]{2,1,0:T(8,128)} %reshape.32.xs_ref, bf16[512,512]{1,0:T(8,128)(2,1)} %all_gather.9.lt_ref, f32[8,512]{1,0:T(8,128)} %bitcast.36, f32[64,4,512]{2,1,0:T(4,128)} %all_gather.11.trades_ref, f32[1,256]{1,0:T(1,128)} %bitcast.41), custom_call_target="tpu_custom_call" | custom-call | tf_op jit(solution)/shard_map/pallas_call | solution.py:156
  174.8 1.0 copy.34
  175.9 0.8 reshape.34
  176.6 3.4 %all-to-all-start.1 = ((f32[8,32,128]{2,1,0:T(8,128)}), f32[8,32,128]{2,1,0:T(8,128)S(1)}, u32[]{:S(2)}, u32[]{:S(2)}) async-start(f32[8,32,128]{2,1,0:T(8,128)} %reshape.34), calls=%async_computation.1 | async-start | bytes 262144 | tf_op jit(solution)/shard_map/all_to_all | solution.py:223
  180.0 0.7 slice.3
  180.7 40.6 %psum.7 = f32[3,64]{1,0:T(4,128)S(1)} all-reduce(f32[3,64]{1,0:T(4,128)S(1)} %slice.3), channel_id=1, replica_groups=mesh['paths'=4,'factors'=8] {'paths','factors'}, use_global_device_ids=true, to_apply=%region_0.1 | all-reduce | flops 192 | bytes 1536 | tf_op jit(solution)/shard_map/psum | solution.py:225
  221.3 0.6 broadcast_multiply_fusion
  221.9 0.1 reshape.35
  222.0 0.2 copy.32
  222.1 0.8 reshape.36
  (23 shorter events, 0.1 us)
Async XLA Ops:
  1.9 0.9 copy-start
  3.1 8.6 %copy-start.7 = (f32[64]{0:T(128)S(1)}, f32[64]{0:T(128)}, u32[]{:S(2)}) copy-start(f32[64]{0:T(128)} %param.19) | copy-start | bytes 772
  3.1 8.6 %copy-start.8 = (f32[64]{0:T(128)S(1)}, f32[64]{0:T(128)}, u32[]{:S(2)}) copy-start(f32[64]{0:T(128)} %param.18) | copy-start | bytes 772
  3.1 8.6 %copy-start.9 = (f32[64]{0:T(128)S(1)}, f32[64]{0:T(128)}, u32[]{:S(2)}) copy-start(f32[64]{0:T(128)} %param.17) | copy-start | bytes 772
  3.1 8.6 %copy-start.10 = (s32[64]{0:T(128)S(1)}, s32[64]{0:T(128)}, u32[]{:S(2)}) copy-start(s32[64]{0:T(128)} %param.20) | copy-start | bytes 772
  3.1 8.7 %copy-start.2 = (s32[4096]{0:T(1024)S(1)}, s32[4096]{0:T(1024)}, u32[]{:S(2)}) copy-start(s32[4096]{0:T(1024)} %param.23) | copy-start | bytes 49156
  3.1 8.7 %copy-start.6 = (f32[64]{0:T(128)S(1)}, f32[64]{0:T(128)}, u32[]{:S(2)}) copy-start(f32[64]{0:T(128)} %param.16) | copy-start | bytes 772
  3.2 48.6 %copy-start.3 = (s32[4096]{0:T(1024)S(1)}, s32[4096]{0:T(1024)}, u32[]{:S(2)}) copy-start(s32[4096]{0:T(1024)} %param.24) | copy-start | bytes 49156
  3.2 48.6 %copy-start.4 = (f32[4096]{0:T(1024)S(1)}, f32[4096]{0:T(1024)}, u32[]{:S(2)}) copy-start(f32[4096]{0:T(1024)} %param.22) | copy-start | bytes 49156
  3.2 48.6 %copy-start.5 = (f32[4096]{0:T(1024)S(1)}, f32[4096]{0:T(1024)}, u32[]{:S(2)}) copy-start(f32[4096]{0:T(1024)} %param.21) | copy-start | bytes 49156
  4.3 47.6 %copy-start.1 = (f32[512,64]{0,1:T(8,128)S(1)}, f32[512,64]{0,1:T(8,128)}, u32[]{:S(2)}) copy-start(f32[512,64]{0,1:T(8,128)} %param.15) | copy-start | bytes 393220
  4.3 114.7 %all-to-all-start = ((f32[8,160,128]{2,1,0:T(8,128)}), f32[8,160,128]{2,1,0:T(8,128)S(1)}, u32[]{:S(2)}, u32[]{:S(2)}) async-start(f32[8,160,128]{2,1,0:T(8,128)} %reshape.30), calls=%async_computation | async-start | bytes 1310720 | tf_op jit(solution)/shard_map/all_to_all | solution.py:216
  176.6 45.2 %all-to-all-start.1 = ((f32[8,32,128]{2,1,0:T(8,128)}), f32[8,32,128]{2,1,0:T(8,128)S(1)}, u32[]{:S(2)}, u32[]{:S(2)}) async-start(f32[8,32,128]{2,1,0:T(8,128)} %reshape.34), calls=%async_computation.1 | async-start | bytes 262144 | tf_op jit(solution)/shard_map/all_to_all | solution.py:223

commit v2 on v1

--- a/solution.py
+++ b/solution.py
@@ -52,8 +52,8 @@
     paths = xs_ref.shape[1]
     blocks, rows, part_width = parts.shape
     width = part_width // 3
-    tiles = trades_ref.shape[0]
-    per_block = tiles // blocks
+    per_block = trades_ref.shape[1] - 1
+    tiles = blocks * per_block
     sets = loss_ref.shape[1]
     slices = g_ref.shape[1]
 
@@ -82,15 +82,15 @@
     exposure[...] = jnp.zeros_like(exposure)
 
     def forward(i, carry):
-        b = i // per_block
-        notional = trades_ref[i, 0:1, :]
-        strike = trades_ref[i, 1:2, :]
-        table = one_hot(trades_ref[i, 3:4, :], width)
+        b, j = i // per_block, i % per_block
+        notional = trades_ref[b, j, 0:1, :]
+        strike = trades_ref[b, j, 1:2, :]
+        table = one_hot(trades_ref[b, j, 3:4, :], width)
         money = mm(parts[b], jnp.concatenate([table, table, table], axis=0), NN) - strike
         squash = jnp.tanh(money)
         value = notional * squash
         slopes[i] = (notional - value * squash).astype(jnp.bfloat16)
-        set_table = one_hot(trades_ref[i, 2:3, :], sets)
+        set_table = one_hot(trades_ref[b, j, 2:3, :], sets)
         exposure[...] += mm(value.astype(jnp.bfloat16), set_table, NT)
         return carry
 
@@ -108,10 +108,10 @@
     terms[...] = jnp.zeros_like(terms)
 
     def backward(i, carry):
-        b = i // per_block
-        set_table = one_hot(trades_ref[i, 2:3, :], sets)
+        b, j = i // per_block, i % per_block
+        set_table = one_hot(trades_ref[b, j, 2:3, :], sets)
         pulled = slopes[i].astype(jnp.float32) * mm(weights, set_table, NN)
-        table = one_hot(trades_ref[i, 3:4, :], width)
+        table = one_hot(trades_ref[b, j, 3:4, :], width)
         terms[b] += mm(pulled.astype(jnp.bfloat16), table, NT)
         return carry
 
@@ -148,10 +148,15 @@
     )
 
 
+def spread(block, axes):
+    copies = jnp.broadcast_to(block[None], (lax.axis_size(axes),) + block.shape)
+    return lax.all_to_all(copies, axes, 0, 0, tiled=True)
+
+
 def local_part(xs, lt, params, trades, loss_given, width, slices):
     steps, paths, factors = xs.shape[0] - 1, xs.shape[1], xs.shape[2]
     blocks = factors // width
-    tiles, _, tile = trades.shape
+    tiles, tile = blocks * (trades.shape[1] - 1), trades.shape[3]
     rows, sets = steps * paths, loss_given.shape[0]
     return pl.pallas_call(
         local_kernel,
@@ -200,16 +205,18 @@
     )
     smile = jnp.dot(jnp.stack([sabr_alpha, sabr_rho, sabr_nu]), slice_table, precision=PRECISE)
     params = jnp.concatenate([smile, reversion[None, :], factor_slice.astype(floats)[None, :]], axis=0)
-    params = jnp.pad(params, ((0, 3), (0, 0)))
-    params = lax.all_gather(params, "factors", axis=1, tiled=True)
+    params = params.reshape(-1)
+    params = jnp.pad(params, (0, 4 * tile - params.shape[0])).reshape(1, 4, tile)
 
     local_factor = trade_factor - lax.axis_index("factors") * width
     trades = jnp.stack(
         [a.astype(floats).reshape(-1, tile) for a in (notional, strike, trade_set, local_factor)],
         axis=1,
     )
-    trades = lax.all_gather(trades, "factors", axis=0, tiled=True)
-    lt = lax.all_gather(cholesky.T.astype(jnp.bfloat16), "factors", axis=0, tiled=True)
+    trades = spread(jnp.concatenate([trades, params], axis=0), "factors")
+    params = trades[:, -1].reshape(groups, -1)[:, : 5 * width].reshape(groups, 5, width)
+    params = params.transpose(1, 0, 2).reshape(5, groups * width)
+    lt = spread(cholesky.T.astype(jnp.bfloat16), "factors").reshape(-1, cholesky.shape[0])
 
     xs = jnp.concatenate([x_start[None], shocks], axis=0)
     xs = xs.reshape(steps + 1, width, groups, paths).transpose(2, 0, 3, 1)
@@ -222,7 +229,7 @@
     back = adjoint.reshape(paths, groups, width).transpose(1, 2, 0)
     back = lax.all_to_all(back.reshape(groups, -1, 128), "factors", 0, 0, tiled=True)
     back = back.reshape(groups, width, paths).transpose(1, 0, 2).reshape(width, path_cols)
-    total = lax.psum(grads[:3], ("paths", "factors"))
+    total = jnp.sum(spread(grads, ("paths", "factors")), axis=0)[:3]
     return back, total / (path_cols * lax.axis_size("paths"))
 
 

time: 223 us -> 149 us (0.67)
  blocking collectives: 147 us -> 0 us
  waiting for transfers between devices: 0.01 us -> 53.1 us
  starting transfers between devices: 10.8 us -> 22.1 us
  other arithmetic: 0.85 us -> 5.23 us
    all_gather x3 -> x0, blocking collectives: 106 us -> none  [the longest x1 39.2 us: per_device(): params = lax.all_gather(params, 'factors', axis=1, tiled=True)]
    psum x1 -> x0, blocking collectives: 40.6 us -> none  [per_device(): total = lax.psum(grads[:3], ('paths', 'factors'))]
    all_to_all x0 -> x3, waiting for transfers between devices: none -> 30.1 us  [spread(): return lax.all_to_all(copies, axes, 0, 0, tiled=True)]
    all_to_all x1, waiting for transfers between devices: 0.01 us -> 17.5 us  [per_device(): lax.all_to_all(xs.reshape(groups, -1, 128), 'factors', 0, 0, tiled=True)]
    all_to_all x0 -> x3, starting transfers between devices: none -> 15.1 us  [spread(): return lax.all_to_all(copies, axes, 0, 0, tiled=True)]
    all_to_all x1, waiting for transfers between devices: 0.01 us -> 5.45 us  [per_device(): lax.all_to_all(back.reshape(groups, -1, 128), 'factors', 0, 0, tiled=True)]
    all_to_all x1, starting transfers between devices: 7.41 us -> 3.64 us  [per_device(): lax.all_to_all(xs.reshape(groups, -1, 128), 'factors', 0, 0, tiled=True)]
    broadcast_in_dim x0 -> x3, local copies, waits for them, and re-layouts: none -> 2.43 us  [spread(): copies = jnp.broadcast_to(block[None], (lax.axis_size(axes),) + block.shape)]
  transfers between devices with their start and end apart: 2 -> 5, of which waited for: 0 -> 5; matrix products, arithmetic and copies ran while one was open for 1% -> 6% of each run, Pallas kernels for 0% -> 0%
where the time goes in v2:
time: 149 us; the launch traced here: 148 us
  Pallas kernels  54.2 us (36%)
  waiting for transfers between devices  53.1 us (36%)
  starting transfers between devices  22.1 us (15%)
  local copies, waits for them, and re-layouts  11.9 us (8%)
  other arithmetic  5.23 us (4%)
    pallas_call x1, Pallas kernels, local_part(): pl.pallas_call(local_kernel, out_shape=(jax.ShapeDtypeStruct((paths, fact...  54.2 us
    all_to_all x3, waiting for transfers between devices, spread(): return lax.all_to_all(copies, axes, 0, 0, tiled=True)  30.1 us
    all_to_all x1, waiting for transfers between devices, per_device(): lax.all_to_all(xs.reshape(groups, -1, 128), 'factors', 0, 0, tiled=True)  17.5 us
    all_to_all x3, starting transfers between devices, spread(): return lax.all_to_all(copies, axes, 0, 0, tiled=True)  15.1 us
    all_to_all x1, waiting for transfers between devices, per_device(): lax.all_to_all(back.reshape(groups, -1, 128), 'factors', 0, 0, tiled=True)  5.45 us
    all_to_all x1, starting transfers between devices, per_device(): lax.all_to_all(xs.reshape(groups, -1, 128), 'factors', 0, 0, tiled=True)  3.64 us
    all_to_all x1, starting transfers between devices, per_device(): lax.all_to_all(back.reshape(groups, -1, 128), 'factors', 0, 0, tiled=True)  3.37 us
  transfers between devices with their start and end apart: 5, of which 5 were waited for; matrix products, arithmetic and copies ran while one was open for 6% of the time, Pallas kernels for 0%

profile of v2, /device:TPU:0, one launch (start us, length us, event | category | flops | bytes accessed | tf_op | source)
XLA Modules:
  0.0 148.2 jit_solution(2235067825681151380)
XLA Ops:
  0.6 0.7 convert_bitcast_fusion.1
  1.4 0.8 fusion
  2.2 0.7 pad_maximum_fusion.1
  3.0 0.7 convert_element_type.20
  3.7 0.7 subtract_convert_fusion
  4.4 0.8 pad_maximum_fusion
  5.2 0.9 broadcast_in_dim.15
  6.1 7.3 %all-to-all-start.2 = ((f32[8,9,4,512]{3,2,1,0:T(4,128)}), f32[8,9,4,512]{3,2,1,0:T(4,128)S(1)}, u32[]{:S(2)}, u32[]{:S(2)}) async-start(f32[8,9,4,512]{3,2,1,0:T(4,128)} %broadcast_in_dim.15), calls=%async_computation.2 | async-start | bytes 1179648 | tf_op jit(solution)/shard_map/all_to_all | solution.py:153
  14.0 0.5 copy-done.2
  14.8 1.1 reshape.48
  15.9 13.4 %all-to-all-done.2.trades_ref = f32[8,9,4,512]{3,2,1,0:T(4,128)S(1)} async-done(((f32[8,9,4,512]{3,2,1,0:T(4,128)}), f32[8,9,4,512]{3,2,1,0:T(4,128)S(1)}, u32[]{:S(2)}, u32[]{:S(2)}) %all-to-all-start.2) | async-done | bytes 589856 | tf_op jit(solution)/shard_map/all_to_all | solution.py:153
  29.3 3.6 %all-to-all-start = ((f32[8,160,128]{2,1,0:T(8,128)}), f32[8,160,128]{2,1,0:T(8,128)S(1)}, u32[]{:S(2)}, u32[]{:S(2)}) async-start(f32[8,160,128]{2,1,0:T(8,128)} %reshape.48), calls=%async_computation | async-start | bytes 1310720 | tf_op jit(solution)/shard_map/all_to_all | solution.py:223
  32.9 17.5 %all-to-all-done = f32[8,160,128]{2,1,0:T(8,128)S(1)} async-done(((f32[8,160,128]{2,1,0:T(8,128)}), f32[8,160,128]{2,1,0:T(8,128)S(1)}, u32[]{:S(2)}, u32[]{:S(2)}) %all-to-all-start) | async-done | bytes 655392 | tf_op jit(solution)/shard_map/all_to_all | solution.py:223
  50.4 0.9 broadcast_in_dim.12
  51.3 4.1 %all-to-all-start.1 = ((bf16[8,64,512]{2,1,0:T(8,128)(2,1)}), bf16[8,64,512]{2,1,0:T(8,128)(2,1)}, u32[]{:S(2)}, u32[]{:S(2)}) async-start(bf16[8,64,512]{2,1,0:T(8,128)(2,1)} %broadcast_in_dim.12), calls=%async_computation.1 | async-start | bytes 1048576 | tf_op jit(solution)/shard_map/all_to_all | solution.py:153
  55.6 0.7 reshape.55.par_ref
  56.5 0.7 copy.29
  57.2 1.2 reshape.50.xs_ref
  58.4 11.3 %all-to-all-done.1 = bf16[8,64,512]{2,1,0:T(8,128)(2,1)} async-done(((bf16[8,64,512]{2,1,0:T(8,128)(2,1)}), bf16[8,64,512]{2,1,0:T(8,128)(2,1)}, u32[]{:S(2)}, u32[]{:S(2)}) %all-to-all-start.1) | async-done | bytes 524320 | tf_op jit(solution)/shard_map/all_to_all | solution.py:153
  69.7 54.2 %shard_map.140 = (f32[64,512]{1,0:T(8,128)}, f32[8,64]{1,0:T(8,128)}) custom-call(f32[5,64,512]{2,1,0:T(8,128)} %reshape.50.xs_ref, bf16[512,512]{1,0:T(8,128)(2,1)} %bitcast.4.lt_ref, f32[5,512]{1,0:T(8,128)} %reshape.55.par_ref, f32[8,9,4,512]{3,2,1,0:T(4,128)} %copy-done, f32[1,256]{1,0:T(1,128)} %bitcast.41), custom_call_target="tpu_custom_call" | custom-call | tf_op jit(solution)/shard_map/pallas_call | solution.py:161
  123.9 0.7 broadcast_in_dim.17
  124.6 0.7 reshape.60
  125.3 3.7 %all-to-all-start.4 = ((f32[32,1,512]{2,1,0:T(1,128)}), f32[32,1,512]{2,1,0:T(1,128)S(1)}, u32[]{:S(2)}, u32[]{:S(2)}) async-start(f32[32,1,512]{2,1,0:T(1,128)} %reshape.60), calls=%async_computation.4 | async-start | bytes 131072 | tf_op jit(solution)/shard_map/all_to_all | solution.py:153
  129.0 1.0 copy.34
  130.0 0.8 reshape.57
  130.8 5.5 %all-to-all-done.4 = f32[32,1,512]{2,1,0:T(1,128)S(1)} async-done(((f32[32,1,512]{2,1,0:T(1,128)}), f32[32,1,512]{2,1,0:T(1,128)S(1)}, u32[]{:S(2)}, u32[]{:S(2)}) %all-to-all-start.4) | async-done | bytes 65568 | tf_op jit(solution)/shard_map/all_to_all | solution.py:153
  136.3 3.4 %all-to-all-start.3 = ((f32[8,32,128]{2,1,0:T(8,128)}), f32[8,32,128]{2,1,0:T(8,128)S(1)}, u32[]{:S(2)}, u32[]{:S(2)}) async-start(f32[8,32,128]{2,1,0:T(8,128)} %reshape.57), calls=%async_computation.3 | async-start | bytes 262144 | tf_op jit(solution)/shard_map/all_to_all | solution.py:230
  139.7 0.5 broadcast.7
  140.2 0.8 reduce
  141.1 0.6 slice_multiply_fusion
  141.7 5.5 %all-to-all-done.3 = f32[8,32,128]{2,1,0:T(8,128)S(1)} async-done(((f32[8,32,128]{2,1,0:T(8,128)}), f32[8,32,128]{2,1,0:T(8,128)S(1)}, u32[]{:S(2)}, u32[]{:S(2)}) %all-to-all-start.3) | async-done | bytes 131104 | tf_op jit(solution)/shard_map/all_to_all | solution.py:230
  147.4 0.8 reshape.59
  (25 shorter events, 1.7 us)
Async XLA Ops:
  0.6 12.8 %copy-start.1 = (f32[4,64,512]{2,1,0:T(8,128)S(1)}, f32[4,64,512]{2,1,0:T(8,128)}, u32[]{:S(2)}) copy-start(f32[4,64,512]{2,1,0:T(8,128)} %param.14) | copy-start | bytes 1572868
  6.1 23.2 %all-to-all-start.2 = ((f32[8,9,4,512]{3,2,1,0:T(4,128)}), f32[8,9,4,512]{3,2,1,0:T(4,128)S(1)}, u32[]{:S(2)}, u32[]{:S(2)}) async-start(f32[8,9,4,512]{3,2,1,0:T(4,128)} %broadcast_in_dim.15), calls=%async_computation.2 | async-start | bytes 1179648 | tf_op jit(solution)/shard_map/all_to_all | solution.py:153
  13.6 0.9 copy-start.2
  14.8 18.1 %copy-start.3 = (f32[512,64]{0,1:T(8,128)S(1)}, f32[512,64]{0,1:T(8,128)}, u32[]{:S(2)}) copy-start(f32[512,64]{0,1:T(8,128)} %param.15) | copy-start | bytes 393220
  29.3 26.1 %copy-start = (f32[8,9,4,512]{3,2,1,0:T(4,128)}, f32[8,9,4,512]{3,2,1,0:T(4,128)S(1)}, u32[]{:S(2)}) copy-start(f32[8,9,4,512]{3,2,1,0:T(4,128)S(1)} %all-to-all-done.2.trades_ref) | copy-start | bytes 1769476
  29.3 21.1 %all-to-all-start = ((f32[8,160,128]{2,1,0:T(8,128)}), f32[8,160,128]{2,1,0:T(8,128)S(1)}, u32[]{:S(2)}, u32[]{:S(2)}) async-start(f32[8,160,128]{2,1,0:T(8,128)} %reshape.48), calls=%async_computation | async-start | bytes 1310720 | tf_op jit(solution)/shard_map/all_to_all | solution.py:223
  51.3 18.4 %all-to-all-start.1 = ((bf16[8,64,512]{2,1,0:T(8,128)(2,1)}), bf16[8,64,512]{2,1,0:T(8,128)(2,1)}, u32[]{:S(2)}, u32[]{:S(2)}) async-start(bf16[8,64,512]{2,1,0:T(8,128)(2,1)} %broadcast_in_dim.12), calls=%async_computation.1 | async-start | bytes 1048576 | tf_op jit(solution)/shard_map/all_to_all | solution.py:153
  125.3 11.0 %all-to-all-start.4 = ((f32[32,1,512]{2,1,0:T(1,128)}), f32[32,1,512]{2,1,0:T(1,128)S(1)}, u32[]{:S(2)}, u32[]{:S(2)}) async-start(f32[32,1,512]{2,1,0:T(1,128)} %reshape.60), calls=%async_computation.4 | async-start | bytes 131072 | tf_op jit(solution)/shard_map/all_to_all | solution.py:153
  136.3 10.9 %all-to-all-start.3 = ((f32[8,32,128]{2,1,0:T(8,128)}), f32[8,32,128]{2,1,0:T(8,128)S(1)}, u32[]{:S(2)}, u32[]{:S(2)}) async-start(f32[8,32,128]{2,1,0:T(8,128)} %reshape.57), calls=%async_computation.3 | async-start | bytes 262144 | tf_op jit(solution)/shard_map/all_to_all | solution.py:230

commit v3 on v2

--- a/solution.py
+++ b/solution.py
@@ -52,7 +52,8 @@
     paths = xs_ref.shape[1]
     blocks, rows, part_width = parts.shape
     width = part_width // 3
-    per_block = trades_ref.shape[1] - 1
+    parts_of, per_part = trades_ref.shape[0], trades_ref.shape[2]
+    per_block = parts_of * per_part
     tiles = blocks * per_block
     sets = loss_ref.shape[1]
     slices = g_ref.shape[1]
@@ -83,14 +84,15 @@
 
     def forward(i, carry):
         b, j = i // per_block, i % per_block
-        notional = trades_ref[b, j, 0:1, :]
-        strike = trades_ref[b, j, 1:2, :]
-        table = one_hot(trades_ref[b, j, 3:4, :], width)
+        trade = trades_ref.at[j // per_part, b, j % per_part]
+        notional = trade[0:1, :]
+        strike = trade[1:2, :]
+        table = one_hot(trade[3:4, :], width)
         money = mm(parts[b], jnp.concatenate([table, table, table], axis=0), NN) - strike
         squash = jnp.tanh(money)
         value = notional * squash
         slopes[i] = (notional - value * squash).astype(jnp.bfloat16)
-        set_table = one_hot(trades_ref[b, j, 2:3, :], sets)
+        set_table = one_hot(trade[2:3, :], sets)
         exposure[...] += mm(value.astype(jnp.bfloat16), set_table, NT)
         return carry
 
@@ -109,9 +111,10 @@
 
     def backward(i, carry):
         b, j = i // per_block, i % per_block
-        set_table = one_hot(trades_ref[b, j, 2:3, :], sets)
+        trade = trades_ref.at[j // per_part, b, j % per_part]
+        set_table = one_hot(trade[2:3, :], sets)
         pulled = slopes[i].astype(jnp.float32) * mm(weights, set_table, NN)
-        table = one_hot(trades_ref[b, j, 3:4, :], width)
+        table = one_hot(trade[3:4, :], width)
         terms[b] += mm(pulled.astype(jnp.bfloat16), table, NT)
         return carry
 
@@ -156,7 +159,7 @@
 def local_part(xs, lt, params, trades, loss_given, width, slices):
     steps, paths, factors = xs.shape[0] - 1, xs.shape[1], xs.shape[2]
     blocks = factors // width
-    tiles, tile = blocks * (trades.shape[1] - 1), trades.shape[3]
+    tiles, tile = blocks * trades.shape[0] * trades.shape[2], trades.shape[4]
     rows, sets = steps * paths, loss_given.shape[0]
     return pl.pallas_call(
         local_kernel,
@@ -175,6 +178,231 @@
         ],
         compiler_params=pltpu.CompilerParams(vmem_limit_bytes=56 * 1024 * 1024),
     )(xs, lt, params, trades, loss_given[None, :])
+
+
+def barrier(groups, me, parts_of, part):
+    sem = pltpu.get_barrier_semaphore()
+    for o in range(1, groups):
+        pl.semaphore_signal(
+            sem, device_id={"factors": lax.rem(me + o, groups)}, device_id_type=pl.DeviceIdType.MESH
+        )
+    for o in range(1, parts_of):
+        pl.semaphore_signal(
+            sem, device_id={"paths": lax.rem(part + o, parts_of)}, device_id_type=pl.DeviceIdType.MESH
+        )
+    pl.semaphore_wait(sem, groups + parts_of - 2)
+
+
+def send(source, target, send_sem, recv_sem, device):
+    copy = pltpu.make_async_remote_copy(
+        src_ref=source,
+        dst_ref=target,
+        send_sem=send_sem,
+        recv_sem=recv_sem,
+        device_id=device,
+        device_id_type=pl.DeviceIdType.MESH,
+    )
+    copy.start()
+    return copy
+
+
+def fold(block):
+    rows = block.shape[0] * block.shape[1] // 128
+    return jnp.concatenate(
+        [block[at : at + rows] for at in range(0, block.shape[0], rows)], axis=1
+    )
+
+
+def unfold(block, width):
+    return jnp.concatenate([block[:, at : at + width] for at in range(0, 128, width)], axis=0)
+
+
+def gather_kernel(
+    groups,
+    parts_of,
+    x_ref,
+    s_ref,
+    par_ref,
+    lt_ref,
+    tr_ref,
+    xs_out,
+    par_out,
+    lt_out,
+    tr_out,
+    xsend,
+    xrecv,
+    ltbuf,
+    own_sem,
+    lt_sem,
+    tr_sem,
+    x_sem,
+    lt2_sem,
+    tr2_sem,
+):
+    me, part = lax.axis_index("factors"), lax.axis_index("paths")
+    width = x_ref.shape[0]
+    paths = x_ref.shape[1] // groups
+    count = s_ref.shape[0] + 1
+    rows = paths * width // 128
+    for a in range(count):
+        turned = (x_ref[...] if a == 0 else s_ref[a - 1]).T
+        for d in range(groups):
+            xsend[d, a * rows : (a + 1) * rows, :] = fold(turned[d * paths : (d + 1) * paths])
+    for d in range(groups):
+        xsend[d, count * rows :, :] = par_ref[...]
+    own = [
+        pltpu.make_async_copy(lt_ref.at[part], ltbuf.at[part, me], own_sem.at[0]),
+        pltpu.make_async_copy(tr_ref.at[part], tr_out.at[part, me], own_sem.at[1]),
+    ]
+    for copy in own:
+        copy.start()
+    barrier(groups, me, parts_of, part)
+    lts, trs, xss = [], [], []
+    for o in range(1, groups):
+        device = {"factors": lax.rem(me + o, groups)}
+        lts.append(send(lt_ref.at[part], ltbuf.at[part, me], lt_sem.at[0, o], lt_sem.at[1, o], device))
+    for o in range(1, groups):
+        device = {"factors": lax.rem(me + o, groups)}
+        trs.append(send(tr_ref.at[part], tr_out.at[part, me], tr_sem.at[0, o], tr_sem.at[1, o], device))
+    for o in range(1, groups):
+        peer = lax.rem(me + o, groups)
+        xss.append(
+            send(xsend.at[peer], xrecv.at[me], x_sem.at[0, o], x_sem.at[1, o], {"factors": peer})
+        )
+    xrecv[me] = xsend[me]
+    for copy in own:
+        copy.wait()
+    for copy in lts:
+        copy.wait_recv()
+    lt2, tr2 = [], []
+    for o in range(1, parts_of):
+        device = {"paths": lax.rem(part + o, parts_of)}
+        lt2.append(send(ltbuf.at[part], ltbuf.at[part], lt2_sem.at[0, o], lt2_sem.at[1, o], device))
+    for copy in trs:
+        copy.wait_recv()
+    for o in range(1, parts_of):
+        device = {"paths": lax.rem(part + o, parts_of)}
+        tr2.append(send(tr_out.at[part], tr_out.at[part], tr2_sem.at[0, o], tr2_sem.at[1, o], device))
+    for copy in xss:
+        copy.wait_recv()
+    for a in range(count):
+        xs_out[a] = jnp.concatenate(
+            [unfold(xrecv[s, a * rows : (a + 1) * rows, :], width) for s in range(groups)], axis=1
+        )
+    par_out[...] = jnp.concatenate(
+        [xrecv[s, count * rows :, :][:, :width] for s in range(groups)], axis=1
+    )
+    for copy in lt2:
+        copy.wait_recv()
+    per = lt_ref.shape[1]
+    for s in range(groups):
+        for q in range(parts_of):
+            at = (s * parts_of + q) * per
+            lt_out[at : at + per, :] = ltbuf[q, s]
+    for copy in tr2:
+        copy.wait_recv()
+    for copy in lts + trs + xss + lt2 + tr2:
+        copy.wait_send()
+
+
+def gather_part(groups, parts_of, x_start, shocks, params, lt, trades):
+    width, path_cols = x_start.shape
+    paths, steps, factors = path_cols // groups, shocks.shape[0], groups * width
+    rows = (steps + 1) * paths * width // 128 + 8
+    vmem = pl.BlockSpec(memory_space=pltpu.VMEM)
+    dma = pltpu.SemaphoreType.DMA
+    return pl.pallas_call(
+        functools.partial(gather_kernel, groups, parts_of),
+        out_shape=(
+            jax.ShapeDtypeStruct((steps + 1, paths, factors), jnp.float32),
+            jax.ShapeDtypeStruct((8, factors), jnp.float32),
+            jax.ShapeDtypeStruct((factors, factors), jnp.bfloat16),
+            jax.ShapeDtypeStruct((parts_of, groups) + trades.shape[1:], jnp.float32),
+        ),
+        in_specs=[vmem] * 5,
+        out_specs=(vmem,) * 4,
+        scratch_shapes=[
+            pltpu.VMEM((groups, rows, 128), jnp.float32),
+            pltpu.VMEM((groups, rows, 128), jnp.float32),
+            pltpu.VMEM((parts_of, groups) + lt.shape[1:], jnp.bfloat16),
+            dma((2,)),
+            dma((2, groups)),
+            dma((2, groups)),
+            dma((2, groups)),
+            dma((2, parts_of)),
+            dma((2, parts_of)),
+        ],
+        compiler_params=pltpu.CompilerParams(
+            collective_id=0, has_side_effects=True, vmem_limit_bytes=32 * 1024 * 1024
+        ),
+    )(x_start, shocks, params, lt, trades)
+
+
+def return_kernel(
+    groups, parts_of, a_ref, g_ref, out_ref, gout_ref, asend, arecv, gbuf, a_sem, g_sem
+):
+    me, part = lax.axis_index("factors"), lax.axis_index("paths")
+    paths = a_ref.shape[0]
+    width = a_ref.shape[1] // groups
+    rows = paths * width // 128
+    turned = a_ref[...].T
+    for d in range(groups):
+        asend[d, :rows, :] = fold(turned[d * width : (d + 1) * width])
+        asend[d, rows:, :] = g_ref[...]
+    barrier(groups, me, parts_of, part)
+    copies = []
+    for o in range(1, groups):
+        peer = lax.rem(me + o, groups)
+        copies.append(
+            send(asend.at[peer], arecv.at[me], a_sem.at[0, o], a_sem.at[1, o], {"factors": peer})
+        )
+    arecv[me] = asend[me]
+    for copy in copies:
+        copy.wait_recv()
+    total = arecv[0, rows:, :]
+    for s in range(1, groups):
+        total = total + arecv[s, rows:, :]
+    gbuf[part] = total
+    sends = []
+    for o in range(1, parts_of):
+        device = {"paths": lax.rem(part + o, parts_of)}
+        sends.append(send(gbuf.at[part], gbuf.at[part], g_sem.at[0, o], g_sem.at[1, o], device))
+    out_ref[...] = jnp.concatenate(
+        [unfold(arecv[s, :rows, :], paths) for s in range(groups)], axis=1
+    )
+    for copy in sends:
+        copy.wait_recv()
+    total = gbuf[0]
+    for s in range(1, parts_of):
+        total = total + gbuf[s]
+    gout_ref[...] = total
+    for copy in copies + sends:
+        copy.wait_send()
+
+
+def return_part(groups, parts_of, adjoint, grads):
+    paths, factors = adjoint.shape
+    width = factors // groups
+    rows = paths * width // 128
+    vmem = pl.BlockSpec(memory_space=pltpu.VMEM)
+    dma = pltpu.SemaphoreType.DMA
+    return pl.pallas_call(
+        functools.partial(return_kernel, groups, parts_of),
+        out_shape=(
+            jax.ShapeDtypeStruct((width, groups * paths), jnp.float32),
+            jax.ShapeDtypeStruct(grads.shape, jnp.float32),
+        ),
+        in_specs=[vmem] * 2,
+        out_specs=(vmem,) * 2,
+        scratch_shapes=[
+            pltpu.VMEM((groups, rows + 8, 128), jnp.float32),
+            pltpu.VMEM((groups, rows + 8, 128), jnp.float32),
+            pltpu.VMEM((parts_of,) + grads.shape, jnp.float32),
+            dma((2, groups)),
+            dma((2, parts_of)),
+        ],
+        compiler_params=pltpu.CompilerParams(collective_id=1, has_side_effects=True),
+    )(adjoint, grads)
 
 
 def per_device(
@@ -205,18 +433,38 @@
     )
     smile = jnp.dot(jnp.stack([sabr_alpha, sabr_rho, sabr_nu]), slice_table, precision=PRECISE)
     params = jnp.concatenate([smile, reversion[None, :], factor_slice.astype(floats)[None, :]], axis=0)
-    params = params.reshape(-1)
-    params = jnp.pad(params, (0, 4 * tile - params.shape[0])).reshape(1, 4, tile)
-
     local_factor = trade_factor - lax.axis_index("factors") * width
     trades = jnp.stack(
         [a.astype(floats).reshape(-1, tile) for a in (notional, strike, trade_set, local_factor)],
         axis=1,
     )
+    lt = cholesky.T.astype(jnp.bfloat16)
+    parts_of = lax.axis_size("paths")
+    if (
+        width == paths
+        and width in (64, 128)
+        and width % (16 * parts_of) == 0
+        and trades.shape[0] % parts_of == 0
+        and slice_count <= 128
+    ):
+        params = jnp.pad(params, ((0, 3), (0, 128 - width)))
+        lt = lt.reshape(parts_of, width // parts_of, -1)
+        trades = trades.reshape(parts_of, -1, 4, tile)
+        xs, params, lt, trades = gather_part(
+            groups, parts_of, x_start, shocks, params, lt, trades
+        )
+        adjoint, grads = local_part(xs, lt, params, trades, loss_given, width, 128)
+        back, total = return_part(groups, parts_of, adjoint, grads)
+        return back, total[:3, :slice_count] / (path_cols * parts_of)
+
+    params = params.reshape(-1)
+    params = jnp.pad(params, (0, 4 * tile - params.shape[0])).reshape(1, 4, tile)
+
     trades = spread(jnp.concatenate([trades, params], axis=0), "factors")
     params = trades[:, -1].reshape(groups, -1)[:, : 5 * width].reshape(groups, 5, width)
     params = params.transpose(1, 0, 2).reshape(5, groups * width)
-    lt = spread(cholesky.T.astype(jnp.bfloat16), "factors").reshape(-1, cholesky.shape[0])
+    trades = trades[:, :-1][None]
+    lt = spread(lt, "factors").reshape(-1, cholesky.shape[0])
 
     xs = jnp.concatenate([x_start[None], shocks], axis=0)
     xs = xs.reshape(steps + 1, width, groups, paths).transpose(2, 0, 3, 1)

time: 149 us -> 108 us (0.72)
  waiting for transfers between devices: 53.1 us -> 0 us
  Pallas kernels: 54.2 us -> 95.7 us
  starting transfers between devices: 22.1 us -> 0 us
  local copies, waits for them, and re-layouts: 11.9 us -> 6.56 us
    all_to_all x5 -> x0, waiting for transfers between devices: 53.1 us -> none  [the longest x3 30.1 us: spread(): return lax.all_to_all(copies, axes, 0, 0, tiled=True)]
    pallas_call x0 -> x2, Pallas kernels: none -> 41 us  [the longest x1 25.2 us: gather_part(): pl.pallas_call(functools.partial(gather_kernel, groups, parts_of), out_sh...]
    all_to_all x5 -> x0, starting transfers between devices: 22.1 us -> none  [the longest x3 15.1 us: spread(): return lax.all_to_all(copies, axes, 0, 0, tiled=True)]
    reshape x11 -> x0, local copies, waits for them, and re-layouts: 5.97 us -> none  [the longest x1 1.16 us: per_device(): xs = xs.reshape(steps + 1, paths, groups * width)]
    unnamed x12 -> x17, local copies, waits for them, and re-layouts: 1.38 us -> 6.56 us
    broadcast_in_dim x3 -> x0, local copies, waits for them, and re-layouts: 2.43 us -> none  [spread(): copies = jnp.broadcast_to(block[None], (lax.axis_size(axes),) + block.shape)]
  transfers between devices with their start and end apart: 5 -> 0, of which waited for: 5 -> 0; matrix products, arithmetic and copies ran while one was open for 6% -> 0% of each run, Pallas kernels for 0% -> 0%
where the time goes in v3:
time: 108 us
  Pallas kernels  95.7 us (89%)
  local copies, waits for them, and re-layouts  6.56 us (6%)
  other arithmetic  4.19 us (4%)
    pallas_call x1, Pallas kernels, local_part(): pl.pallas_call(local_kernel, out_shape=(jax.ShapeDtypeStruct((paths, fact...  54.7 us
    pallas_call x1, Pallas kernels, gather_part(): pl.pallas_call(functools.partial(gather_kernel, groups, parts_of), out_sh...  25.2 us
    pallas_call x1, Pallas kernels, return_part(): pl.pallas_call(functools.partial(return_kernel, groups, parts_of), out_sh...  15.7 us
    unnamed x17, local copies, waits for them, and re-layouts  6.56 us

profile of v3, /device:TPU:0, one launch (start us, length us, event | category | flops | bytes accessed | tf_op | source)
XLA Modules:
  0.0 108.0 jit_solution(9184311225326245379)
XLA Ops:
  0.6 0.0 copy-start.7
  0.6 0.0 copy-start.6
  0.7 0.7 convert_bitcast_fusion
  1.3 0.8 fusion
  2.2 0.7 select_maximum_fusion.par_ref
  2.9 0.0 copy-done.7
  2.9 0.7 convert_element_type.21
  3.6 0.8 pad_maximum_fusion.tr_ref
  4.4 0.0 copy-done.6
  4.4 0.0 copy-start.4
  4.5 0.9 copy-done.4
  5.3 0.0 copy-start.3
  5.3 1.0 copy-done.3
  6.4 25.2 %shard_map.140 = (f32[5,64,512]{2,1,0:T(8,128)S(1)}, f32[8,512]{1,0:T(8,128)S(1)}, bf16[512,512]{1,0:T(8,128)(2,1)S(1)}, f32[4,8,2,4,512]{4,3,2,1,0:T(4,128)S(1)}) custom-call(f32[64,512]{1,0:T(8,128)S(1)} %copy-done.4, f32[4,64,512]{2,1,0:T(8,128)S(1)} %copy-done.3, f32[8,128]{1,0:T(8,128)S(1)} %select_maximum_fusion.par_ref, ...), custom_call_target="tpu_custom_call" | custom-call | tf_op jit(solution)/shard_map/pallas_call | solution.py:314
  31.6 0.0 copy-start
  31.6 0.8 copy-done
  32.4 0.0 copy-start.1
  32.5 0.8 copy-done.1
  33.2 0.0 copy-start.2
  33.3 0.8 copy-done.2
  34.1 0.0 copy-start.5
  34.1 0.6 copy-done.5
  34.7 54.7 %shard_map.141 = (f32[64,512]{1,0:T(8,128)}, f32[8,128]{1,0:T(8,128)}) custom-call(f32[5,64,512]{2,1,0:T(8,128)} %copy-done, bf16[512,512]{1,0:T(8,128)(2,1)} %copy-done.1, f32[8,512]{1,0:T(8,128)} %copy-done.5, f32[4,8,2,4,512]{4,3,2,1,0:T(4,128)} %copy-done.2, f32[1,256]{1,0:T(1,128)} %bitcast.19), custom_call_target="tpu_custom_call" | custom-call | tf_op jit(solution)/shard_map/pallas_call | solution.py:164
  89.4 15.7 %shard_map.142 = (f32[64,512]{1,0:T(8,128)}, f32[8,128]{1,0:T(8,128)}) custom-call(f32[64,512]{1,0:T(8,128)} %get-tuple-element.14.a_ref, f32[8,128]{1,0:T(8,128)} %get-tuple-element.15.g_ref), custom_call_target="tpu_custom_call" | custom-call | tf_op jit(solution)/shard_map/pallas_call | solution.py:389
  105.1 1.3 %slice_multiply_fusion = f32[3,64]{1,0:T(4,128)} fusion(f32[8,128]{1,0:T(8,128)} %get-tuple-element.17), kind=kLoop, calls=%fused_computation.14 | loop fusion | flops 192 | bytes 1536 | tf_op jit(solution)/shard_map/div | solution.py:458
  106.4 1.6 %copy.16 = f32[64,512]{1,0:T(8,128)} copy(f32[64,512]{1,0:T(8,128)} %get-tuple-element.20) | data formatting | bytes 262144
  (2 shorter events, 0.0 us)
Async XLA Ops:
  0.6 2.2 %copy-start.7 = (s32[4096]{0:T(1024)S(1)}, s32[4096]{0:T(1024)}, u32[]{:S(2)}) copy-start(s32[4096]{0:T(1024)} %param.24) | copy-start | bytes 49156
  0.6 3.8 %copy-start.6 = (f32[512,64]{0,1:T(8,128)S(1)}, f32[512,64]{0,1:T(8,128)}, u32[]{:S(2)}) copy-start(f32[512,64]{0,1:T(8,128)} %param.15) | copy-start | bytes 393220
  4.4 0.9 copy-start.4
  5.3 1.0 copy-start.3
  31.6 0.8 copy-start
  32.4 0.8 copy-start.1
  33.2 0.8 copy-start.2
  34.1 0.6 copy-start.5

commit v4 on v3

--- a/solution.py
+++ b/solution.py
@@ -14,7 +14,8 @@
 PRECISE = lax.Precision.HIGHEST
 NN = (((1,), (0,)), ((), ()))
 NT = (((1,), (1,)), ((), ()))
-TILE = 512
+TILE = 1024
+UNROLL = 4
 
 
 def mm(a, b, dims):
@@ -30,8 +31,13 @@
 
 
 def one_hot(ids, count):
-    rows = lax.broadcasted_iota(jnp.int32, (count, ids.shape[1]), 0).astype(jnp.float32)
-    return jnp.where(rows == ids, 1.0, 0.0).astype(jnp.bfloat16)
+    shape = (16, ids.shape[1])
+    near = jnp.broadcast_to(ids, shape).astype(jnp.int32) - lax.broadcasted_iota(jnp.int32, shape, 0)
+    near = near.astype(jnp.int16)
+    one, zero = jnp.ones(shape, jnp.bfloat16), jnp.zeros(shape, jnp.bfloat16)
+    return jnp.concatenate(
+        [jnp.where(near == jnp.int16(at), one, zero) for at in range(0, count, 16)], axis=0
+    )
 
 
 def local_kernel(
@@ -96,7 +102,7 @@
         exposure[...] += mm(value.astype(jnp.bfloat16), set_table, NT)
         return carry
 
-    lax.fori_loop(0, tiles, forward, 0)
+    lax.fori_loop(0, tiles, forward, 0, unroll=UNROLL)
 
     weights = jnp.concatenate(
         [
@@ -118,7 +124,7 @@
         terms[b] += mm(pulled.astype(jnp.bfloat16), table, NT)
         return carry
 
-    lax.fori_loop(0, tiles, backward, 0)
+    lax.fori_loop(0, tiles, backward, 0, unroll=UNROLL)
 
     adjoint = jnp.zeros_like(state)
     sums = [jnp.zeros((1, state.shape[1]), jnp.float32) for _ in range(3)]

time: 108 us -> 79.9 us (0.74)
  Pallas kernels: 95.7 us -> 67.2 us
    pallas_call x1, Pallas kernels: 54.7 us -> 26.2 us  [local_part(): pl.pallas_call(local_kernel, out_shape=(jax.ShapeDtypeStruct((paths, fact...]
where the time goes in v4:
time: 79.9 us; the launch traced here: 79.4 us
  Pallas kernels  67.2 us (84%)
  local copies, waits for them, and re-layouts  6.56 us (8%)
  other arithmetic  4.19 us (5%)
  matrix products  0.83 us (1%)
    pallas_call x1, Pallas kernels, local_part(): pl.pallas_call(local_kernel, out_shape=(jax.ShapeDtypeStruct((paths, fact...  26.2 us
    pallas_call x1, Pallas kernels, gather_part(): pl.pallas_call(functools.partial(gather_kernel, groups, parts_of), out_sh...  25.2 us
    pallas_call x1, Pallas kernels, return_part(): pl.pallas_call(functools.partial(return_kernel, groups, parts_of), out_sh...  15.7 us
    unnamed x17, local copies, waits for them, and re-layouts  6.56 us

profile of v4, /device:TPU:0, one launch (start us, length us, event | category | flops | bytes accessed | tf_op | source)
XLA Modules:
  0.0 79.4 jit_solution(10424358550308996055)
XLA Ops:
  0.6 0.0 copy-start.7
  0.6 0.0 copy-start.6
  0.7 0.7 convert_bitcast_fusion
  1.3 0.8 %fusion = f32[3,64]{1,0:T(4,128)S(1)} fusion(s32[64]{0:T(128)} %param.20, f32[1,64]{1,0:T(1,128)} %bitcast.23, f32[1,64]{1,0:T(1,128)} %bitcast.24, f32[1,64]{1,0:T(1,128)} %bitcast.25), kind=kOutput, calls=%fused_computation.2 | convolution fusion | flops 151936 | bytes 1792 | tf_op jit(solution)/shard_map/dot_general | solution.py:440
  2.2 0.7 select_maximum_fusion.par_ref
  2.9 0.0 copy-done.7
  2.9 0.7 convert_element_type.21
  3.6 0.8 %maximum_bitcast_fusion.tr_ref = f32[4,1,4,1024]{3,2,1,0:T(4,128)S(1)} fusion(f32[4,1,1024]{2,1,0:T(1,128)S(1)} %bitcast.17, f32[4,1,1024]{2,1,0:T(1,128)S(1)} %bitcast.18, f32[4,1,1024]{2,1,0:T(1,128)} %bitcast.19, f32[4,1,1024]{2,1,0:T(1,128)} %bitcast.20), kind=kLoop, calls=%fused_computation | loop fusion | flops 49152 | bytes 131072 | tf_op jit(solution)/shard_map/reshape | solution.py:458
  4.4 0.0 copy-done.6
  4.4 0.0 copy-start.4
  4.5 0.9 %copy-done.4 = f32[64,512]{1,0:T(8,128)S(1)} copy-done((f32[64,512]{1,0:T(8,128)S(1)}, f32[64,512]{1,0:T(8,128)}, u32[]{:S(2)}) %copy-start.4) | copy-done | bytes 131096
  5.3 0.0 copy-start.3
  5.3 1.0 %copy-done.3 = f32[4,64,512]{2,1,0:T(8,128)S(1)} copy-done((f32[4,64,512]{2,1,0:T(8,128)S(1)}, f32[4,64,512]{2,1,0:T(8,128)}, u32[]{:S(2)}) %copy-start.3) | copy-done | bytes 524312
  6.4 25.2 %shard_map.140 = (f32[5,64,512]{2,1,0:T(8,128)S(1)}, f32[8,512]{1,0:T(8,128)S(1)}, bf16[512,512]{1,0:T(8,128)(2,1)S(1)}, f32[4,8,1,4,1024]{4,3,2,1,0:T(4,128)S(1)}) custom-call(f32[64,512]{1,0:T(8,128)S(1)} %copy-done.4, f32[4,64,512]{2,1,0:T(8,128)S(1)} %copy-done.3, f32[8,128]{1,0:T(8,128)S(1)} %select_maximum_fusion.par_ref, ...), custom_call_target="tpu_custom_call" | custom-call | tf_op jit(solution)/shard_map/pallas_call | solution.py:320
  31.6 0.0 copy-start
  31.6 0.8 %copy-done = f32[5,64,512]{2,1,0:T(8,128)} copy-done((f32[5,64,512]{2,1,0:T(8,128)}, f32[5,64,512]{2,1,0:T(8,128)S(1)}, u32[]{:S(2)}) %copy-start) | copy-done | bytes 655384
  32.4 0.0 copy-start.1
  32.5 0.8 %copy-done.1 = bf16[512,512]{1,0:T(8,128)(2,1)} copy-done((bf16[512,512]{1,0:T(8,128)(2,1)}, bf16[512,512]{1,0:T(8,128)(2,1)S(1)}, u32[]{:S(2)}) %copy-start.1) | copy-done | bytes 524312
  33.2 0.0 copy-start.2
  33.3 0.8 %copy-done.2 = f32[4,8,1,4,1024]{4,3,2,1,0:T(4,128)} copy-done((f32[4,8,1,4,1024]{4,3,2,1,0:T(4,128)}, f32[4,8,1,4,1024]{4,3,2,1,0:T(4,128)S(1)}, u32[]{:S(2)}) %copy-start.2) | copy-done | bytes 524312
  34.1 0.0 copy-start.5
  34.1 0.6 copy-done.5
  34.7 26.2 %shard_map.141 = (f32[64,512]{1,0:T(8,128)}, f32[8,128]{1,0:T(8,128)}) custom-call(f32[5,64,512]{2,1,0:T(8,128)} %copy-done, bf16[512,512]{1,0:T(8,128)(2,1)} %copy-done.1, f32[8,512]{1,0:T(8,128)} %copy-done.5, f32[4,8,1,4,1024]{4,3,2,1,0:T(4,128)} %copy-done.2, f32[1,256]{1,0:T(1,128)} %bitcast.21), custom_call_target="tpu_custom_call" | custom-call | tf_op jit(solution)/shard_map/pallas_call | solution.py:170
  60.9 15.7 %shard_map.142 = (f32[64,512]{1,0:T(8,128)}, f32[8,128]{1,0:T(8,128)}) custom-call(f32[64,512]{1,0:T(8,128)} %get-tuple-element.14.a_ref, f32[8,128]{1,0:T(8,128)} %get-tuple-element.15.g_ref), custom_call_target="tpu_custom_call" | custom-call | tf_op jit(solution)/shard_map/pallas_call | solution.py:395
  76.6 1.3 %slice_multiply_fusion = f32[3,64]{1,0:T(4,128)} fusion(f32[8,128]{1,0:T(8,128)} %get-tuple-element.17), kind=kLoop, calls=%fused_computation.14 | loop fusion | flops 192 | bytes 1536 | tf_op jit(solution)/shard_map/div | solution.py:464
  77.9 1.6 %copy.16 = f32[64,512]{1,0:T(8,128)} copy(f32[64,512]{1,0:T(8,128)} %get-tuple-element.20) | data formatting | bytes 262144
  (2 shorter events, 0.0 us)
Async XLA Ops:
  0.6 2.2 %copy-start.7 = (s32[4096]{0:T(1024)S(1)}, s32[4096]{0:T(1024)}, u32[]{:S(2)}) copy-start(s32[4096]{0:T(1024)} %param.24) | copy-start | bytes 49156
  0.6 3.8 %copy-start.6 = (f32[512,64]{0,1:T(8,128)S(1)}, f32[512,64]{0,1:T(8,128)}, u32[]{:S(2)}) copy-start(f32[512,64]{0,1:T(8,128)} %param.15) | copy-start | bytes 393220
  4.4 0.9 %copy-start.4 = (f32[64,512]{1,0:T(8,128)S(1)}, f32[64,512]{1,0:T(8,128)}, u32[]{:S(2)}) copy-start(f32[64,512]{1,0:T(8,128)} %x_ref.1) | copy-start | bytes 393220
  5.3 1.0 %copy-start.3 = (f32[4,64,512]{2,1,0:T(8,128)S(1)}, f32[4,64,512]{2,1,0:T(8,128)}, u32[]{:S(2)}) copy-start(f32[4,64,512]{2,1,0:T(8,128)} %s_ref.1) | copy-start | bytes 1572868
  31.6 0.8 %copy-start = (f32[5,64,512]{2,1,0:T(8,128)}, f32[5,64,512]{2,1,0:T(8,128)S(1)}, u32[]{:S(2)}) copy-start(f32[5,64,512]{2,1,0:T(8,128)S(1)} %get-tuple-element.10.xs_ref) | copy-start | bytes 1966084
  32.4 0.8 %copy-start.1 = (bf16[512,512]{1,0:T(8,128)(2,1)}, bf16[512,512]{1,0:T(8,128)(2,1)S(1)}, u32[]{:S(2)}) copy-start(bf16[512,512]{1,0:T(8,128)(2,1)S(1)} %get-tuple-element.11.lt_ref) | copy-start | bytes 1572868
  33.2 0.8 %copy-start.2 = (f32[4,8,1,4,1024]{4,3,2,1,0:T(4,128)}, f32[4,8,1,4,1024]{4,3,2,1,0:T(4,128)S(1)}, u32[]{:S(2)}) copy-start(f32[4,8,1,4,1024]{4,3,2,1,0:T(4,128)S(1)} %get-tuple-element.13.trades_ref) | copy-start | bytes 1572868
  34.1 0.6 copy-start.5

commit v5 on v4

--- a/solution.py
+++ b/solution.py
@@ -196,7 +196,7 @@
         pl.semaphore_signal(
             sem, device_id={"paths": lax.rem(part + o, parts_of)}, device_id_type=pl.DeviceIdType.MESH
         )
-    pl.semaphore_wait(sem, groups + parts_of - 2)
+    return functools.partial(pl.semaphore_wait, sem, groups + parts_of - 2)
 
 
 def send(source, target, send_sem, recv_sem, device):
@@ -262,7 +262,7 @@
     ]
     for copy in own:
         copy.start()
-    barrier(groups, me, parts_of, part)
+    barrier(groups, me, parts_of, part)()
     lts, trs, xss = [], [], []
     for o in range(1, groups):
         device = {"factors": lax.rem(me + o, groups)}
@@ -345,9 +345,34 @@
 
 
 def return_kernel(
-    groups, parts_of, a_ref, g_ref, out_ref, gout_ref, asend, arecv, gbuf, a_sem, g_sem
+    groups,
+    parts_of,
+    xs_ref,
+    lt_ref,
+    par_ref,
+    trades_ref,
+    loss_ref,
+    out_ref,
+    gout_ref,
+    states,
+    parts,
+    slopes,
+    exposure,
+    terms,
+    a_ref,
+    g_ref,
+    asend,
+    arecv,
+    gbuf,
+    a_sem,
+    g_sem,
 ):
     me, part = lax.axis_index("factors"), lax.axis_index("paths")
+    all_in = barrier(groups, me, parts_of, part)
+    local_kernel(
+        xs_ref, lt_ref, par_ref, trades_ref, loss_ref, a_ref, g_ref,
+        states, parts, slopes, exposure, terms,
+    )
     paths = a_ref.shape[0]
     width = a_ref.shape[1] // groups
     rows = paths * width // 128
@@ -355,7 +380,7 @@
     for d in range(groups):
         asend[d, :rows, :] = fold(turned[d * width : (d + 1) * width])
         asend[d, rows:, :] = g_ref[...]
-    barrier(groups, me, parts_of, part)
+    all_in()
     copies = []
     for o in range(1, groups):
         peer = lax.rem(me + o, groups)
@@ -386,29 +411,40 @@
         copy.wait_send()
 
 
-def return_part(groups, parts_of, adjoint, grads):
-    paths, factors = adjoint.shape
+def return_part(groups, parts_of, xs, lt, params, trades, loss_given):
+    paths, factors = xs.shape[1], xs.shape[2]
     width = factors // groups
     rows = paths * width // 128
+    batch, sets = (xs.shape[0] - 1) * paths, loss_given.shape[0]
+    tiles, tile = groups * trades.shape[0] * trades.shape[2], trades.shape[4]
     vmem = pl.BlockSpec(memory_space=pltpu.VMEM)
     dma = pltpu.SemaphoreType.DMA
     return pl.pallas_call(
         functools.partial(return_kernel, groups, parts_of),
         out_shape=(
             jax.ShapeDtypeStruct((width, groups * paths), jnp.float32),
-            jax.ShapeDtypeStruct(grads.shape, jnp.float32),
+            jax.ShapeDtypeStruct((8, 128), jnp.float32),
         ),
-        in_specs=[vmem] * 2,
+        in_specs=[vmem] * 5,
         out_specs=(vmem,) * 2,
         scratch_shapes=[
+            pltpu.VMEM((xs.shape[0] - 1, paths, factors), jnp.float32),
+            pltpu.VMEM((groups, batch, 3 * width), jnp.bfloat16),
+            pltpu.VMEM((tiles, batch, tile), jnp.bfloat16),
+            pltpu.VMEM((batch, sets), jnp.float32),
+            pltpu.VMEM((groups, batch, width), jnp.float32),
+            pltpu.VMEM((paths, factors), jnp.float32),
+            pltpu.VMEM((8, 128), jnp.float32),
             pltpu.VMEM((groups, rows + 8, 128), jnp.float32),
             pltpu.VMEM((groups, rows + 8, 128), jnp.float32),
-            pltpu.VMEM((parts_of,) + grads.shape, jnp.float32),
+            pltpu.VMEM((parts_of, 8, 128), jnp.float32),
             dma((2, groups)),
             dma((2, parts_of)),
         ],
-        compiler_params=pltpu.CompilerParams(collective_id=1, has_side_effects=True),
-    )(adjoint, grads)
+        compiler_params=pltpu.CompilerParams(
+            collective_id=1, has_side_effects=True, vmem_limit_bytes=56 * 1024 * 1024
+        ),
+    )(xs, lt, params, trades, loss_given[None, :])
 
 
 def per_device(
@@ -459,8 +495,7 @@
         xs, params, lt, trades = gather_part(
             groups, parts_of, x_start, shocks, params, lt, trades
         )
-        adjoint, grads = local_part(xs, lt, params, trades, loss_given, width, 128)
-        back, total = return_part(groups, parts_of, adjoint, grads)
+        back, total = return_part(groups, parts_of, xs, lt, params, trades, loss_given)
         return back, total[:3, :slice_count] / (path_cols * parts_of)
 
     params = params.reshape(-1)

time: 79.9 us -> 76.6 us (0.959)
  Pallas kernels: 67.2 us -> 63.8 us
    pallas_call x1 -> x0, Pallas kernels: 26.2 us -> none  [local_part(): pl.pallas_call(local_kernel, out_shape=(jax.ShapeDtypeStruct((paths, fact...]
    pallas_call x1, Pallas kernels: 15.7 us -> 38.6 us  [return_part(): pl.pallas_call(functools.partial(return_kernel, groups, parts_of), out_sh...]
where the time goes in v5:
time: 76.6 us; the launch traced here: 76.1 us
  Pallas kernels  63.8 us (83%)
  local copies, waits for them, and re-layouts  6.55 us (9%)
  other arithmetic  4.19 us (5%)
  matrix products  0.83 us (1%)
    pallas_call x1, Pallas kernels, return_part(): pl.pallas_call(functools.partial(return_kernel, groups, parts_of), out_sh...  38.6 us
    pallas_call x1, Pallas kernels, gather_part(): pl.pallas_call(functools.partial(gather_kernel, groups, parts_of), out_sh...  25.2 us
    unnamed x17, local copies, waits for them, and re-layouts  6.55 us

profile of v5, /device:TPU:0, one launch (start us, length us, event | category | flops | bytes accessed | tf_op | source)
XLA Modules:
  0.0 76.1 jit_solution(11644346001185540182)
XLA Ops:
  0.6 0.0 copy-start.7
  0.6 0.0 copy-start.6
  0.7 0.7 convert_bitcast_fusion
  1.3 0.8 %fusion = f32[3,64]{1,0:T(4,128)S(1)} fusion(s32[64]{0:T(128)} %param.20, f32[1,64]{1,0:T(1,128)} %bitcast.23, f32[1,64]{1,0:T(1,128)} %bitcast.24, f32[1,64]{1,0:T(1,128)} %bitcast.25), kind=kOutput, calls=%fused_computation.2 | convolution fusion | flops 151936 | bytes 1792 | tf_op jit(solution)/shard_map/dot_general | solution.py:476
  2.2 0.7 select_maximum_fusion.par_ref
  2.9 0.0 copy-done.7
  2.9 0.7 convert_element_type.21
  3.6 0.8 %maximum_bitcast_fusion.tr_ref = f32[4,1,4,1024]{3,2,1,0:T(4,128)S(1)} fusion(f32[4,1,1024]{2,1,0:T(1,128)S(1)} %bitcast.17, f32[4,1,1024]{2,1,0:T(1,128)S(1)} %bitcast.18, f32[4,1,1024]{2,1,0:T(1,128)} %bitcast.19, f32[4,1,1024]{2,1,0:T(1,128)} %bitcast.20), kind=kLoop, calls=%fused_computation | loop fusion | flops 49152 | bytes 131072 | tf_op jit(solution)/shard_map/reshape | solution.py:494
  4.4 0.0 copy-done.6
  4.4 0.0 copy-start.4
  4.5 0.9 %copy-done.4 = f32[64,512]{1,0:T(8,128)S(1)} copy-done((f32[64,512]{1,0:T(8,128)S(1)}, f32[64,512]{1,0:T(8,128)}, u32[]{:S(2)}) %copy-start.4) | copy-done | bytes 131096
  5.3 0.0 copy-start.3
  5.3 1.0 %copy-done.3 = f32[4,64,512]{2,1,0:T(8,128)S(1)} copy-done((f32[4,64,512]{2,1,0:T(8,128)S(1)}, f32[4,64,512]{2,1,0:T(8,128)}, u32[]{:S(2)}) %copy-start.3) | copy-done | bytes 524312
  6.4 25.2 %shard_map.140 = (f32[5,64,512]{2,1,0:T(8,128)S(1)}, f32[8,512]{1,0:T(8,128)S(1)}, bf16[512,512]{1,0:T(8,128)(2,1)S(1)}, f32[4,8,1,4,1024]{4,3,2,1,0:T(4,128)S(1)}) custom-call(f32[64,512]{1,0:T(8,128)S(1)} %copy-done.4, f32[4,64,512]{2,1,0:T(8,128)S(1)} %copy-done.3, f32[8,128]{1,0:T(8,128)S(1)} %select_maximum_fusion.par_ref, ...), custom_call_target="tpu_custom_call" | custom-call | tf_op jit(solution)/shard_map/pallas_call | solution.py:320
  31.6 0.0 copy-start
  31.6 0.8 %copy-done = f32[5,64,512]{2,1,0:T(8,128)} copy-done((f32[5,64,512]{2,1,0:T(8,128)}, f32[5,64,512]{2,1,0:T(8,128)S(1)}, u32[]{:S(2)}) %copy-start) | copy-done | bytes 655384
  32.4 0.0 copy-start.1
  32.4 0.8 %copy-done.1 = bf16[512,512]{1,0:T(8,128)(2,1)} copy-done((bf16[512,512]{1,0:T(8,128)(2,1)}, bf16[512,512]{1,0:T(8,128)(2,1)S(1)}, u32[]{:S(2)}) %copy-start.1) | copy-done | bytes 524312
  33.2 0.0 copy-start.2
  33.2 0.8 %copy-done.2 = f32[4,8,1,4,1024]{4,3,2,1,0:T(4,128)} copy-done((f32[4,8,1,4,1024]{4,3,2,1,0:T(4,128)}, f32[4,8,1,4,1024]{4,3,2,1,0:T(4,128)S(1)}, u32[]{:S(2)}) %copy-start.2) | copy-done | bytes 524312
  34.1 0.0 copy-start.5
  34.1 0.6 copy-done.5
  34.7 38.6 %shard_map.141 = (f32[64,512]{1,0:T(8,128)}, f32[8,128]{1,0:T(8,128)}) custom-call(f32[5,64,512]{2,1,0:T(8,128)} %copy-done, bf16[512,512]{1,0:T(8,128)(2,1)} %copy-done.1, f32[8,512]{1,0:T(8,128)} %copy-done.5, f32[4,8,1,4,1024]{4,3,2,1,0:T(4,128)} %copy-done.2, f32[1,256]{1,0:T(1,128)} %bitcast.21), custom_call_target="tpu_custom_call" | custom-call | tf_op jit(solution)/shard_map/pallas_call | solution.py:422
  73.3 1.3 %slice_multiply_fusion = f32[3,64]{1,0:T(4,128)} fusion(f32[8,128]{1,0:T(8,128)} %get-tuple-element.13), kind=kLoop, calls=%fused_computation.14 | loop fusion | flops 192 | bytes 1536 | tf_op jit(solution)/shard_map/div | solution.py:499
  74.5 1.6 %copy.16 = f32[64,512]{1,0:T(8,128)} copy(f32[64,512]{1,0:T(8,128)} %get-tuple-element.16) | data formatting | bytes 262144
  (2 shorter events, 0.0 us)
Async XLA Ops:
  0.6 2.2 %copy-start.7 = (s32[4096]{0:T(1024)S(1)}, s32[4096]{0:T(1024)}, u32[]{:S(2)}) copy-start(s32[4096]{0:T(1024)} %param.24) | copy-start | bytes 49156
  0.6 3.8 %copy-start.6 = (f32[512,64]{0,1:T(8,128)S(1)}, f32[512,64]{0,1:T(8,128)}, u32[]{:S(2)}) copy-start(f32[512,64]{0,1:T(8,128)} %param.15) | copy-start | bytes 393220
  4.4 0.9 %copy-start.4 = (f32[64,512]{1,0:T(8,128)S(1)}, f32[64,512]{1,0:T(8,128)}, u32[]{:S(2)}) copy-start(f32[64,512]{1,0:T(8,128)} %x_ref.1) | copy-start | bytes 393220
  5.3 1.0 %copy-start.3 = (f32[4,64,512]{2,1,0:T(8,128)S(1)}, f32[4,64,512]{2,1,0:T(8,128)}, u32[]{:S(2)}) copy-start(f32[4,64,512]{2,1,0:T(8,128)} %s_ref.1) | copy-start | bytes 1572868
  31.6 0.8 %copy-start = (f32[5,64,512]{2,1,0:T(8,128)}, f32[5,64,512]{2,1,0:T(8,128)S(1)}, u32[]{:S(2)}) copy-start(f32[5,64,512]{2,1,0:T(8,128)S(1)} %get-tuple-element.8.xs_ref) | copy-start | bytes 1966084
  32.4 0.8 %copy-start.1 = (bf16[512,512]{1,0:T(8,128)(2,1)}, bf16[512,512]{1,0:T(8,128)(2,1)S(1)}, u32[]{:S(2)}) copy-start(bf16[512,512]{1,0:T(8,128)(2,1)S(1)} %get-tuple-element.9.lt_ref) | copy-start | bytes 1572868
  33.2 0.8 %copy-start.2 = (f32[4,8,1,4,1024]{4,3,2,1,0:T(4,128)}, f32[4,8,1,4,1024]{4,3,2,1,0:T(4,128)S(1)}, u32[]{:S(2)}) copy-start(f32[4,8,1,4,1024]{4,3,2,1,0:T(4,128)S(1)} %get-tuple-element.11.trades_ref) | copy-start | bytes 1572868
  34.1 0.6 copy-start.5
